TPU v7x, 32 devices: a whole 2x2x4 slice. The times are simulated.
32 devices in a mesh: dp: 8 (over y, x, core), mp: 4 (over z).
Axes of the slice: x: 2, y: 2, z: 4, core: 2. Of those that a mesh axis runs over, the one named last changes fastest.
Arguments:
- hidden_rows: bfloat16 [4096, 3584], P('dp'), may hold values from -6 to 6
- key_grad: bfloat16 [4096, 512], P('dp', 'mp'), may hold values from -6 to 6
- value_grad: bfloat16 [4096, 512], P('dp', 'mp'), may hold values from -6 to 6
- visual_rows: bfloat16 [2048, 1024], P('dp'), may hold values from -6 to 6
- visual_cotangent: bfloat16 [8, 4, 64, 3584], P('dp'), may hold values from -6 to 6
- norm_gain: float32 [1024], replicated, may hold values from 0.25 to 1.75
- norm_bias: float32 [1024], replicated, may hold values from -3 to 3
- fc1_weight: bfloat16 [1024, 4096], P(None, 'mp'), may hold values from -0.1875 to 0.1875
- fc1_bias: float32 [4096], P('mp'), may hold values from -3 to 3
- fc2_weight: bfloat16 [4096, 1024], P('mp'), may hold values from -0.09375 to 0.09375
- fc2_bias: float32 [1024], replicated, may hold values from -3 to 3
- layer_scale: float32 [1024], replicated, may hold values from 0.3 to 1.5
- token_counts: int32 [8, 8], P('dp'), may hold values from 1 to 32, as said below
- dest_offsets: int32 [8, 8], P('dp'), may hold values from 1 to 4, as said below
Outputs:
- key_weight_grad: float32 [3592, 512], P('dp', 'mp')
- value_weight_grad: float32 [3592, 512], P('dp', 'mp')
- projector_grad: float32 [3592, 1024], P('dp', 'mp')
- handoff: bfloat16 [8, 4, 64, 1024], P('dp', None, None, 'mp')
Inputs may be any that keep to these rules, and one draw needn't show every extreme that they name: `token_counts`: on every data rank the images of one distance, chosen per rank, all have 32 rows. `dest_offsets`: every data rank sends exactly 2 images to each distance from 1 to 4.
All inputs are finite; a program needn't handle non-finite values.
Results may differ from a plain program's by a relative error of at most 0.0046.
Values may be sent and summed in bfloat16 or wider, within the bound.
No kernel may reach another device: no remote copies, remote signals or barrier semaphores. Data moves between devices by JAX's collectives and lax.ppermute only.
A program may use at most 64 MiB of HBM per device.

v0:
```python
import jax
import jax.numpy as jnp
from jax import lax
from jax.sharding import PartitionSpec as P

SPREAD = 4
CAP = 64


def shifted(x, axis, by):
    count = lax.axis_size(axis)
    return lax.ppermute(x, axis, [(i, (i + by) % count) for i in range(count)])


def pack_rows(rows, counts, offsets):
    total_rows = rows.shape[0]
    images = counts.shape[0]
    ends = jnp.cumsum(counts)
    starts = ends - counts
    places = jnp.arange(total_rows)
    image_ids = jnp.arange(images)
    owner = jnp.sum((places[:, None] >= ends[None, :]).astype(jnp.int32), axis=1)
    member = (owner[:, None] == image_ids[None, :]).astype(jnp.int32)
    earlier = (image_ids[None, :] < image_ids[:, None]) & (offsets[None, :] == offsets[:, None])
    before = jnp.sum(earlier.astype(jnp.int32) * counts[None, :], axis=1)
    row_dest = jnp.sum(member * offsets[None, :], axis=1)
    row_start = jnp.sum(member * starts[None, :], axis=1)
    row_before = jnp.sum(member * before[None, :], axis=1)
    slot_index = row_before + places - row_start
    target = jnp.where(places < ends[images - 1], (row_dest - 1) * CAP + slot_index, -1)
    slot_ids = jnp.arange(SPREAD * CAP)
    select = (slot_ids[:, None] == target[None, :]).astype(jnp.bfloat16)
    packed = jnp.dot(select, rows, preferred_element_type=jnp.float32).astype(jnp.bfloat16)
    return packed.reshape(SPREAD, CAP, rows.shape[1])


def vision(
    visual_rows,
    norm_gain,
    norm_bias,
    fc1_weight,
    fc1_bias,
    fc2_weight,
    fc2_bias,
    layer_scale,
    token_counts,
    dest_offsets,
):
    values = visual_rows.astype(jnp.float32)
    center = jnp.mean(values, axis=1, keepdims=True)
    spread_sq = jnp.mean((values - center) ** 2, axis=1, keepdims=True)
    normed = ((values - center) * lax.rsqrt(spread_sq + 1e-06) * norm_gain + norm_bias).astype(
        jnp.bfloat16
    )
    hidden = jax.nn.gelu(
        jnp.dot(normed, fc1_weight, preferred_element_type=jnp.float32) + fc1_bias,
        approximate=False,
    ).astype(jnp.bfloat16)
    partial_value = jnp.dot(hidden, fc2_weight, preferred_element_type=jnp.float32)
    summed = lax.psum_scatter(partial_value, "mp", scatter_dimension=1, tiled=True)
    column_count = summed.shape[1]
    first_col = lax.axis_index("mp") * column_count
    own_values = lax.dynamic_slice_in_dim(values, first_col, column_count, 1)
    own_scale = lax.dynamic_slice_in_dim(layer_scale, first_col, column_count, 0)
    own_bias = lax.dynamic_slice_in_dim(fc2_bias, first_col, column_count, 0)
    encoded = (own_values + own_scale * (summed + own_bias)).astype(jnp.bfloat16)
    packed = pack_rows(encoded, token_counts[0], dest_offsets[0])
    received = []
    for distance in range(SPREAD):
        received.append(shifted(packed[distance], "dp", distance + 1))
    return jnp.stack(received, axis=0)[None]


def per_device(
    hidden_rows,
    key_grad,
    value_grad,
    visual_rows,
    visual_cotangent,
    norm_gain,
    norm_bias,
    fc1_weight,
    fc1_bias,
    fc2_weight,
    fc2_bias,
    layer_scale,
    token_counts,
    dest_offsets,
):
    tokens_here, width = hidden_rows.shape
    devices = lax.axis_size("dp")
    shard_rows = (width + devices) // devices
    padded_width = shard_rows * devices
    ones_column = jnp.ones((tokens_here, 1), jnp.bfloat16)
    zero_columns = jnp.zeros((tokens_here, padded_width - width - 1), jnp.bfloat16)
    augmented = jnp.concatenate([hidden_rows, ones_column, zero_columns], axis=1)
    key_cols = key_grad.shape[1]
    kv_cotangent = jnp.concatenate([key_grad, value_grad], axis=1)

    def make_projector(handoff):
        slot_count = handoff.shape[1] * handoff.shape[2]
        cot_flat = visual_cotangent.reshape(slot_count, width)
        cot_padded = jnp.concatenate(
            [cot_flat, jnp.zeros((slot_count, padded_width - width), jnp.bfloat16)], axis=1
        )
        received_rows = handoff.reshape(slot_count, handoff.shape[3])

        def projector_rows(start, count):
            return lax.dot_general(
                cot_padded,
                received_rows,
                (((0,), (0,)), ((), ())),
                preferred_element_type=jnp.float32,
            )

        return projector_rows

    kv_results = lax.psum_scatter(
        lax.dot_general(
            augmented, kv_cotangent, (((0,), (0,)), ((), ())), preferred_element_type=jnp.float32
        ),
        "dp",
        scatter_dimension=0,
        tiled=True,
    )
    key_weight_grad = kv_results[:, :key_cols]
    value_weight_grad = kv_results[:, key_cols:]
    handoff = vision(
        visual_rows,
        norm_gain,
        norm_bias,
        fc1_weight,
        fc1_bias,
        fc2_weight,
        fc2_bias,
        layer_scale,
        token_counts,
        dest_offsets,
    )
    projector_rows = make_projector(handoff)
    projector_grad = lax.psum_scatter(
        projector_rows(jnp.int32(0), lax.axis_size("dp") * shard_rows),
        "dp",
        scatter_dimension=0,
        tiled=True,
    )
    return (key_weight_grad, value_weight_grad, projector_grad, handoff)


def solution(mesh):
    placed = (
        P("dp", None),
        P("dp", "mp"),
        P("dp", "mp"),
        P("dp", None),
        P("dp", None, None, None),
        P(),
        P(),
        P(None, "mp"),
        P("mp"),
        P("mp", None),
        P(),
        P(),
        P("dp", None),
        P("dp", None),
    )
    return jax.shard_map(
        per_device,
        mesh=mesh,
        in_specs=placed,
        out_specs=(P("dp", "mp"), P("dp", "mp"), P("dp", "mp"), P("dp", None, None, "mp")),
        check_vma=False,
    )
```

profile of v0, /device:TPU:0, one launch (start us, length us, event | category | flops | bytes accessed | tf_op | source)
XLA Modules:
  0.0 158.1 jit_solution(14281039852675778282)
XLA Ops:
  8.0 0.0 copy-start
  8.0 0.0 reduce-scatter.4.cloned.1.call-start
  8.1 1.3 convert_reduce_fusion
  9.4 1.3 multiply_reduce_fusion
  10.7 0.0 copy-done
  10.7 0.0 copy-start.1
  10.8 0.0 copy-start.6
  10.8 6.3 %fusion.13 = f32[256,1024]{1,0:T(8,128)} fusion(bf16[1024,1024]{1,0:T(8,128)(2,1)S(1)} %copy-done, bf16[1024,1024]{1,0:T(8,128)(2,1)} %param.21, bf16[256,1024]{1,0:T(8,128)(2,1)} %param.17, f32[1024]{0:T(1024)} %param.22, f32[1024]{0:T(1024)} %param.20, f32[1024]{0:T(1024)} %param.19, f32[256]{0:T(256)S(1)} %add_rsqrt_fusion, ...), kind=kOutput, calls=%fused_computation.25 | convolution fusion | flops 1092616192 | bytes 5781504 | tf_op jit(solution)/shard_map/dot_general | solution.py:59
  17.1 0.0 reduce-scatter.4.cloned.1.call-update
  17.1 0.0 all-reduce.6.cloned.1.call-start
  17.1 0.0 copy-done.1
  17.1 1.1 convert_element_type.22
  18.3 0.8 dynamic_slice.11
  19.0 0.8 dynamic_slice.10
  19.8 0.0 copy-done.6
  19.8 0.2 reduce-window.4
  20.0 0.6 slice.28
  20.6 0.0 copy-start.4
  20.6 0.0 copy-start.2
  20.6 0.0 copy-start.3
  20.7 6.7 %concatenate.9 = bf16[512,3592]{1,0:T(8,128)(2,1)} concatenate(bf16[512,3584]{1,0:T(8,128)(2,1)} %param.14, bf16[512,1]{1,0:T(8,128)(2,1)S(1)} %broadcast_in_dim.7, bf16[512,7]{1,0:T(8,128)(2,1)S(1)} %broadcast_in_dim.8), dimensions={1} | concatenate | bytes 7356416 | tf_op jit(solution)/shard_map/concatenate | solution.py:96
  27.3 0.1 convert_reduce_fusion.1
  27.4 0.0 copy-done.4
  27.4 0.2 select_reduce_fusion.3
  27.6 0.1 select_reduce_fusion.2
  27.7 0.7 compare_select_fusion
  28.3 18.9 %reduce-scatter.4.cloned.1.call-done = f32[256,256]{1,0:T(8,128)} async-done(((f32[256,1024]{1,0:T(8,128)}), f32[256,256]{1,0:T(8,128)}) %reduce-scatter.4.cloned.1.call-update) | async-done | bytes 262160 | tf_op jit(solution)/shard_map/reduce_scatter | solution.py:60
  47.2 1.2 convolution_convert_fusion
  48.5 1.6 collective-permute-start.3
  50.0 0.2 collective-permute-start.2
  50.3 1.2 collective-permute-start.1
  51.5 0.4 collective-permute-start
  51.9 0.0 copy-done.2
  51.9 0.0 copy-done.3
  51.9 5.1 %fusion.53 = f32[3592,256]{1,0:T(8,128)} fusion(bf16[512,3592]{1,0:T(8,128)(2,1)} %concatenate.9, bf16[512,128]{1,0:T(8,128)(2,1)S(1)} %copy-done.2, bf16[512,128]{1,0:T(8,128)(2,1)S(1)} %copy-done.3), kind=kOutput, calls=%fused_computation.62 | convolution fusion | flops 942145536 | bytes 7618560 | tf_op jit(solution)/shard_map/dot_general | solution.py:119
  57.0 0.0 copy-start.5
  57.0 0.0 all-reduce.6.cloned.1.call-update
  57.0 0.6 copy-done.5
  57.6 0.6 fusion.98
  59.5 0.0 collective-permute-done.3
  59.5 0.0 collective-permute-done.2
  59.5 0.0 collective-permute-done.1
  59.6 0.0 collective-permute-done
  59.6 0.7 fusion.95
  60.2 4.5 %fusion.1 = f32[3592,256]{1,0:T(8,128)} fusion(bf16[256,256]{1,0:T(8,128)(2,1)S(1)} %bitcast.27, bf16[256,3584]{1,0:T(8,128)(2,1)} %bitcast.26), kind=kOutput, calls=%fused_computation | convolution fusion | flops 470810624 | bytes 5644288 | tf_op jit(solution)/shard_map/dot_general | solution.py:109
  64.7 57.2 %fusion = f32[456,256]{1,0:T(8,128)S(1)} fusion(f32[3592,256]{1,0:T(8,128)} %fusion.1), kind=kCustom, calls=%all-reduce-scatter | all-reduce-scatter fusion | flops 933889 | bytes 4145664
  121.9 1.3 collective-permute-start.4
  123.2 24.2 %all-reduce.6.cloned.1.call-done = f32[3592,256]{1,0:T(8,128)} async-done(((f32[3592,256]{1,0:T(8,128)}), f32[3592,256]{1,0:T(8,128)}) %all-reduce.6.cloned.1.call-update) | async-done | bytes 3678224
  147.5 1.9 %fusion.96 = (f32[449,128]{1,0:T(8,128)}, f32[449,128]{1,0:T(8,128)}) fusion(f32[3592,256]{1,0:T(8,128)} %all-reduce.6.cloned.1.call-done, u32[]{:T(128)S(6)} %multiply.13, u32[]{:T(128)S(6)} %convert), kind=kLoop, calls=%fused_computation.122 | loop fusion | bytes 919560 | tf_op jit(solution)/shard_map/slice | solution.py:127
  149.4 0.0 collective-permute-done.4
  149.4 0.5 concatenate.12
  149.9 0.8 constant_dynamic-slice_fusion
  (7 shorter events, 0.1 us)
Async XLA Ops:
  8.0 2.7 %copy-start = (bf16[1024,1024]{1,0:T(8,128)(2,1)S(1)}, bf16[1024,1024]{1,0:T(8,128)(2,1)}, u32[]{:S(2)}) copy-start(bf16[1024,1024]{1,0:T(8,128)(2,1)} %param.23) | copy-start | bytes 6291460
  8.0 39.2 %reduce-scatter.4.cloned.1.call-start = ((), (), s32[]{:S(2)}) async-start(), calls=%async_computation.1 | async-start | bytes 1310720 | tf_op jit(solution)/shard_map/reduce_scatter | solution.py:60
  10.7 6.4 %copy-start.1 = (bf16[256,1024]{1,0:T(8,128)(2,1)S(1)}, bf16[256,1024]{1,0:T(8,128)(2,1)}, u32[]{:S(2)}) copy-start(bf16[256,1024]{1,0:T(8,128)(2,1)} %param.17) | copy-start | bytes 1572868
  10.8 9.0 %copy-start.6 = (s32[1,8]{1,0:T(1,128)S(1)}, s32[1,8]{1,0:T(1,128)}, u32[]{:S(2)}) copy-start(s32[1,8]{1,0:T(1,128)} %param.26) | copy-start | bytes 100
  17.1 130.4 %all-reduce.6.cloned.1.call-start = ((), (), s32[]{:S(2)}) async-start(), calls=%async_computation.2 | async-start | bytes 7356416
  20.6 6.8 %copy-start.4 = (s32[1,8]{1,0:T(1,128)S(1)}, s32[1,8]{1,0:T(1,128)}, u32[]{:S(2)}) copy-start(s32[1,8]{1,0:T(1,128)} %param.27) | copy-start | bytes 100
  20.6 31.3 %copy-start.2 = (bf16[512,128]{1,0:T(8,128)(2,1)S(1)}, bf16[512,128]{1,0:T(8,128)(2,1)}, u32[]{:S(2)}) copy-start(bf16[512,128]{1,0:T(8,128)(2,1)} %param.16) | copy-start | bytes 393220
  20.6 31.3 %copy-start.3 = (bf16[512,128]{1,0:T(8,128)(2,1)S(1)}, bf16[512,128]{1,0:T(8,128)(2,1)}, u32[]{:S(2)}) copy-start(bf16[512,128]{1,0:T(8,128)(2,1)} %param.15) | copy-start | bytes 393220
  48.5 11.0 %collective-permute-start.3 = (bf16[64,256]{1,0:T(8,128)(2,1)S(1)}, bf16[64,256]{1,0:T(8,128)(2,1)S(1)}, u32[]{:S(2)}, u32[]{:S(2)}) collective-permute-start(bf16[64,256]{1,0:T(8,128)(2,1)S(1)} %get-tuple-element.12), channel_id=1, source_target_pairs={{0,16},{4,20},{8,24},{12,28},{16,0},{20,4},{24,8},{28,12},{1,17},{... | collective-permute-start | bytes 98312 | tf_op jit(solution)/shard_map/ppermute | solution.py:12
  50.0 9.5 %collective-permute-start.2 = (bf16[64,256]{1,0:T(8,128)(2,1)S(1)}, bf16[64,256]{1,0:T(8,128)(2,1)S(1)}, u32[]{:S(2)}, u32[]{:S(2)}) collective-permute-start(bf16[64,256]{1,0:T(8,128)(2,1)S(1)} %get-tuple-element.13), channel_id=1, source_target_pairs={{0,12},{4,16},{8,20},{12,24},{16,28},{20,0},{24,4},{28,8},{1,13},{... | collective-permute-start | bytes 98312 | tf_op jit(solution)/shard_map/ppermute | solution.py:12
  50.3 9.3 %collective-permute-start.1 = (bf16[64,256]{1,0:T(8,128)(2,1)S(1)}, bf16[64,256]{1,0:T(8,128)(2,1)S(1)}, u32[]{:S(2)}, u32[]{:S(2)}) collective-permute-start(bf16[64,256]{1,0:T(8,128)(2,1)S(1)} %get-tuple-element.14), channel_id=1, source_target_pairs={{0,8},{4,12},{8,16},{12,20},{16,24},{20,28},{24,0},{28,4},{1,9},{5... | collective-permute-start | bytes 98312 | tf_op jit(solution)/shard_map/ppermute | solution.py:12
  51.5 8.0 %collective-permute-start = (bf16[64,256]{1,0:T(8,128)(2,1)S(1)}, bf16[64,256]{1,0:T(8,128)(2,1)S(1)}, u32[]{:S(2)}, u32[]{:S(2)}) collective-permute-start(bf16[64,256]{1,0:T(8,128)(2,1)S(1)} %get-tuple-element.11), channel_id=1, source_target_pairs={{0,4},{4,8},{8,12},{12,16},{16,20},{20,24},{24,28},{28,0},{1,5},{5... | collective-permute-start | bytes 98312 | tf_op jit(solution)/shard_map/ppermute | solution.py:12
  57.0 0.7 copy-start.5
  121.9 27.4 %collective-permute-start.4 = (f32[49,256]{1,0:T(8,128)S(1)}, f32[49,256]{1,0:T(8,128)S(1)}, u32[]{:S(2)}, u32[]{:S(2)}) collective-permute-start(f32[49,256]{1,0:T(8,128)S(1)} %slice.37), channel_id=1, source_target_pairs={{0,4},{4,8},{8,12},{12,16},{16,20},{20,24},{24,28},{1,5},{5,9},{9,... | collective-permute-start | bytes 150536
Sparse Core Ops, SparseCore 0:
  17.2 29.9 reduce-scatter.3
Sparse Core Ops, SparseCore 1:
  57.1 90.3 all-reduce.5
where the time goes:
time: 159 us; the launch traced here: 158 us
  blocking collectives  57.2 us (36%)
  waiting for transfers between devices  43.2 us (27%)
  matrix products  17.1 us (11%)
  between operations  17 us (11%)
  local copies, waits for them, and re-layouts  13.3 us (8%)
  other arithmetic  5.67 us (4%)
  starting transfers between devices  4.79 us (3%)
    unnamed x1, blocking collectives  57.2 us
    unnamed x4, waiting for transfers between devices  24.3 us
    reduce_scatter x1, waiting for transfers between devices, vision(): lax.psum_scatter(partial_value, 'mp', scatter_dimension=1, tiled=True)  18.9 us
    concatenate x1, local copies, waits for them, and re-layouts, per_device(): jnp.concatenate([hidden_rows, ones_column, zero_columns], axis=1)  6.67 us
    dot_general x1, matrix products, vision(): jnp.dot(hidden, fc2_weight, preferred_element_type=jnp.float32)  6.29 us
    dot_general x1, matrix products, per_device(): lax.dot_general(augmented, kv_cotangent, (((0,), (0,)), ((), ())), prefer...  5.07 us
    dot_general x1, matrix products, projector_rows(): lax.dot_general(cot_padded, received_rows, (((0,), (0,)), ((), ())), pref...  4.49 us
    ppermute x4, starting transfers between devices, shifted(): return lax.ppermute(x, axis, [(i, (i + by) % count) for i in range(count)])  3.41 us
  transfers between devices with their start and end apart: 7, of which 2 were waited for; matrix products, arithmetic and copies ran while one was open for 51% of the time, Pallas kernels for 0%

commit v1 on v0

--- a/solution.py
+++ b/solution.py
@@ -1,10 +1,139 @@
+from functools import partial
+
 import jax
 import jax.numpy as jnp
 from jax import lax
+from jax.experimental import pallas as pl
+from jax.experimental.pallas import tpu as pltpu
 from jax.sharding import PartitionSpec as P
 
 SPREAD = 4
 CAP = 64
+FEW = 8
+CHUNK = 512
+
+
+def chip_shift(x, by):
+    count = lax.axis_size("dp")
+    return lax.ppermute(x, "dp", [(i, (i + 2 * by) % count) for i in range(count)])
+
+
+def core_swap(x):
+    count = lax.axis_size("dp")
+    return lax.ppermute(x, "dp", [(i, i ^ 1) for i in range(count)])
+
+
+def partial_kernel(core_ref, left_ref, right_ref, keep_ref, send_ref, total_ref, *, ranks, rows, width, ones_row):
+    step = pl.program_id(0)
+    chunk = left_ref.shape[1]
+    right = right_ref[...]
+    total_ref[pl.ds(pl.multiple_of(step * chunk, 8), chunk), :] = lax.dot_general(
+        left_ref[...], right, (((0,), (0,)), ((), ())), preferred_element_type=jnp.float32
+    )
+
+    @pl.when(step == pl.num_programs(0) - 1)
+    def _():
+        extra = total_ref.shape[0] - width
+        if ones_row:
+            first = lax.broadcasted_iota(jnp.int32, (extra, right.shape[0]), 0) == 0
+            picked = jnp.where(first, 1.0, 0.0).astype(jnp.bfloat16)
+            total_ref[width:, :] = jnp.dot(picked, right, preferred_element_type=jnp.float32)
+        else:
+            total_ref[width:, :] = jnp.zeros((extra, right.shape[1]), jnp.float32)
+        for core in range(2):
+
+            @pl.when(core_ref[0] == core)
+            def _():
+                for rank in range(ranks):
+                    piece = total_ref[rank * rows : (rank + 1) * rows, :].astype(jnp.bfloat16)
+                    if rank % 2 == core:
+                        keep_ref[rank // 2] = piece
+                    else:
+                        send_ref[rank // 2] = piece
+
+
+def partial_blocks(left, right, ranks, rows, ones_row):
+    tokens, width = left.shape
+    cols = right.shape[1]
+    chunk = CHUNK if width % CHUNK == 0 else width
+    core = jnp.reshape(lax.axis_index("dp") % 2, (1,)).astype(jnp.int32)
+    block = jax.ShapeDtypeStruct((ranks // 2, rows, cols), jnp.bfloat16)
+    whole = pl.BlockSpec((ranks // 2, rows, cols), lambda i, s: (0, 0, 0))
+    return pl.pallas_call(
+        partial(partial_kernel, ranks=ranks, rows=rows, width=width, ones_row=ones_row),
+        out_shape=(block, block),
+        grid_spec=pltpu.PrefetchScalarGridSpec(
+            num_scalar_prefetch=1,
+            grid=(width // chunk,),
+            in_specs=[
+                pl.BlockSpec((tokens, chunk), lambda i, s: (0, i)),
+                pl.BlockSpec((tokens, cols), lambda i, s: (0, 0)),
+            ],
+            out_specs=(whole, whole),
+            scratch_shapes=[pltpu.VMEM((ranks * rows, cols), jnp.float32)],
+        ),
+        name="partial_kv" if ones_row else "partial_proj",
+    )(core, left, right)
+
+
+def chip_sum_kernel(chip_ref, keep_ref, got_ref, own_ref, *send_refs):
+    chips = keep_ref.shape[0]
+    for distance in range(chips):
+        target = lax.rem(chip_ref[0] + distance, chips)
+        total = keep_ref[target].astype(jnp.float32) + got_ref[target].astype(jnp.float32)
+        if distance == 0:
+            own_ref[...] = total
+        else:
+            send_refs[distance - 1][...] = total.astype(jnp.bfloat16)
+
+
+def chip_sums(keep, got, name):
+    chips, rows, cols = keep.shape
+    chip = jnp.reshape(lax.axis_index("dp") // 2, (1,)).astype(jnp.int32)
+    return pl.pallas_call(
+        chip_sum_kernel,
+        in_specs=[
+            pl.BlockSpec(memory_space=pltpu.SMEM),
+            pl.BlockSpec(memory_space=pltpu.VMEM),
+            pl.BlockSpec(memory_space=pltpu.VMEM),
+        ],
+        out_shape=(jax.ShapeDtypeStruct((rows, cols), jnp.float32),)
+        + (jax.ShapeDtypeStruct((rows, cols), jnp.bfloat16),) * (chips - 1),
+        name=name,
+    )(chip, keep, got)
+
+
+def reduced_rows(left, right, ranks, rows, ones_row):
+    if ranks <= FEW and ranks % 2 == 0:
+        keep, send = partial_blocks(left, right, ranks, rows, ones_row)
+        got = core_swap(send)
+        own, *sends = chip_sums(keep, got, "chip_kv" if ones_row else "chip_proj")
+        total = own
+        for distance, block in enumerate(sends, 1):
+            total = total + chip_shift(block, distance).astype(jnp.float32)
+        return total
+    tokens, width = left.shape
+    filler = jnp.zeros((tokens, ranks * rows - width), jnp.bfloat16)
+    if ones_row:
+        filler = filler.at[:, 0].set(1)
+    padded = jnp.concatenate([left, filler], axis=1)
+    product = lax.dot_general(padded, right, (((0,), (0,)), ((), ())), preferred_element_type=jnp.float32)
+    return lax.psum_scatter(product, "dp", scatter_dimension=0, tiled=True)
+
+
+def feature_sum(value):
+    shards = lax.axis_size("mp")
+    rows, width = value.shape
+    cols = width // shards
+    if shards > FEW:
+        return lax.psum_scatter(value, "mp", scatter_dimension=1, tiled=True)
+    me = lax.axis_index("mp")
+    total = lax.dynamic_slice_in_dim(value, me * cols, cols, 1)
+    narrow = value.astype(jnp.bfloat16)
+    for distance in range(1, shards):
+        piece = lax.dynamic_slice_in_dim(narrow, ((me + distance) % shards) * cols, cols, 1)
+        total = total + shifted(piece, "mp", distance).astype(jnp.float32)
+    return total
 
 
 def shifted(x, axis, by):
@@ -57,7 +186,7 @@
         approximate=False,
     ).astype(jnp.bfloat16)
     partial_value = jnp.dot(hidden, fc2_weight, preferred_element_type=jnp.float32)
-    summed = lax.psum_scatter(partial_value, "mp", scatter_dimension=1, tiled=True)
+    summed = feature_sum(partial_value)
     column_count = summed.shape[1]
     first_col = lax.axis_index("mp") * column_count
     own_values = lax.dynamic_slice_in_dim(values, first_col, column_count, 1)
@@ -87,42 +216,12 @@
     token_counts,
     dest_offsets,
 ):
-    tokens_here, width = hidden_rows.shape
+    width = hidden_rows.shape[1]
     devices = lax.axis_size("dp")
     shard_rows = (width + devices) // devices
-    padded_width = shard_rows * devices
-    ones_column = jnp.ones((tokens_here, 1), jnp.bfloat16)
-    zero_columns = jnp.zeros((tokens_here, padded_width - width - 1), jnp.bfloat16)
-    augmented = jnp.concatenate([hidden_rows, ones_column, zero_columns], axis=1)
     key_cols = key_grad.shape[1]
     kv_cotangent = jnp.concatenate([key_grad, value_grad], axis=1)
-
-    def make_projector(handoff):
-        slot_count = handoff.shape[1] * handoff.shape[2]
-        cot_flat = visual_cotangent.reshape(slot_count, width)
-        cot_padded = jnp.concatenate(
-            [cot_flat, jnp.zeros((slot_count, padded_width - width), jnp.bfloat16)], axis=1
-        )
-        received_rows = handoff.reshape(slot_count, handoff.shape[3])
-
-        def projector_rows(start, count):
-            return lax.dot_general(
-                cot_padded,
-                received_rows,
-                (((0,), (0,)), ((), ())),
-                preferred_element_type=jnp.float32,
-            )
-
-        return projector_rows
-
-    kv_results = lax.psum_scatter(
-        lax.dot_general(
-            augmented, kv_cotangent, (((0,), (0,)), ((), ())), preferred_element_type=jnp.float32
-        ),
-        "dp",
-        scatter_dimension=0,
-        tiled=True,
-    )
+    kv_results = reduced_rows(hidden_rows, kv_cotangent, devices, shard_rows, True)
     key_weight_grad = kv_results[:, :key_cols]
     value_weight_grad = kv_results[:, key_cols:]
     handoff = vision(
@@ -137,13 +236,10 @@
         token_counts,
         dest_offsets,
     )
-    projector_rows = make_projector(handoff)
-    projector_grad = lax.psum_scatter(
-        projector_rows(jnp.int32(0), lax.axis_size("dp") * shard_rows),
-        "dp",
-        scatter_dimension=0,
-        tiled=True,
-    )
+    slot_count = handoff.shape[1] * handoff.shape[2]
+    cotangent = visual_cotangent.reshape(slot_count, width)
+    received_rows = handoff.reshape(slot_count, handoff.shape[3])
+    projector_grad = reduced_rows(cotangent, received_rows, devices, shard_rows, False)
     return (key_weight_grad, value_weight_grad, projector_grad, handoff)
 
 

time: 159 us -> 82.7 us (0.52)
  blocking collectives: 57.2 us -> 0 us
  waiting for transfers between devices: 43.2 us -> 14.1 us
  Pallas kernels: 0 us -> 19.4 us
  between operations: 17 us -> 0.84 us
  starting transfers between devices: 4.79 us -> 18.5 us
  matrix products: 17.1 us -> 7.72 us
  other arithmetic: 5.67 us -> 8.7 us
    unnamed x1 -> x0, blocking collectives: 57.2 us -> none
    unnamed x4 -> x0, waiting for transfers between devices: 24.3 us -> none
    pallas_call x0 -> x4, Pallas kernels: none -> 19.4 us  [the longest x2 14.2 us: partial_blocks(): pl.pallas_call(partial(partial_kernel, ranks=ranks, rows=rows, width=widt...]
    reduce_scatter x1 -> x0, waiting for transfers between devices: 18.9 us -> none  [vision(): lax.psum_scatter(partial_value, 'mp', scatter_dimension=1, tiled=True)]
    ppermute x0 -> x8, waiting for transfers between devices: none -> 10.7 us  [the longest x6 10.7 us: chip_shift(): lax.ppermute(x, 'dp', [(i, (i + 2 * by) % count) for i in range(count)])]
    dot_general x2 -> x0, matrix products: 9.56 us -> none  [the longest x1 5.07 us: per_device(): lax.dot_general(augmented, kv_cotangent, (((0,), (0,)), ((), ())), prefer...]
    ppermute x0 -> x8, starting transfers between devices: none -> 7.95 us  [the longest x6 7.88 us: chip_shift(): lax.ppermute(x, 'dp', [(i, (i + 2 * by) % count) for i in range(count)])]
    ppermute x4 -> x7, starting transfers between devices: 3.41 us -> 10.6 us  [shifted(): return lax.ppermute(x, axis, [(i, (i + by) % count) for i in range(count)])]
  transfers between devices with their start and end apart: 7 -> 15, of which waited for: 2 -> 7; matrix products, arithmetic and copies ran while one was open for 51% -> 22% of each run, Pallas kernels for 0% -> 24%
where the time goes in v1:
time: 82.7 us; the launch traced here: 82 us
  Pallas kernels  19.4 us (23%)
  starting transfers between devices  18.5 us (22%)
  waiting for transfers between devices  14.1 us (17%)
  local copies, waits for them, and re-layouts  12.8 us (15%)
  other arithmetic  8.7 us (11%)
  matrix products  7.72 us (9%)
  between operations  0.84 us (1%)
    pallas_call x2, Pallas kernels, partial_blocks(): pl.pallas_call(partial(partial_kernel, ranks=ranks, rows=rows, width=widt...  14.2 us
    ppermute x6, waiting for transfers between devices, chip_shift(): lax.ppermute(x, 'dp', [(i, (i + 2 * by) % count) for i in range(count)])  10.7 us
    ppermute x7, starting transfers between devices, shifted(): return lax.ppermute(x, axis, [(i, (i + by) % count) for i in range(count)])  10.6 us
    ppermute x6, starting transfers between devices, chip_shift(): lax.ppermute(x, 'dp', [(i, (i + 2 * by) % count) for i in range(count)])  7.88 us
    dot_general x1, matrix products, vision(): jnp.dot(hidden, fc2_weight, preferred_element_type=jnp.float32)  6.26 us
    pallas_call x2, Pallas kernels, chip_sums(): pl.pallas_call(chip_sum_kernel, in_specs=[pl.BlockSpec(memory_space=pltpu...  5.18 us
    ppermute x2, local copies, waits for them, and re-layouts, core_swap(): return lax.ppermute(x, 'dp', [(i, i ^ 1) for i in range(count)])  4.53 us
    pallas_call x2, local copies, waits for them, and re-layouts, partial_blocks(): pl.pallas_call(partial(partial_kernel, ranks=ranks, rows=rows, width=widt...  4.02 us
  transfers between devices with their start and end apart: 15, of which 7 were waited for; matrix products, arithmetic and copies ran while one was open for 22% of the time, Pallas kernels for 24%

profile of v1, /device:TPU:0, one launch (start us, length us, event | category | flops | bytes accessed | tf_op | source)
XLA Modules:
  0.0 82.0 jit_solution(14067126426756234314)
XLA Ops:
  0.6 0.0 copy-start
  0.7 1.3 %convert_reduce_fusion = f32[256]{0:T(256)S(1)} fusion(bf16[256,1024]{1,0:T(8,128)(2,1)} %param.17), kind=kLoop, calls=%fused_computation.24 | loop fusion | flops 524032 | bytes 525312 | tf_op jit(solution)/shard_map/reduce_sum | solution.py:179
  2.0 1.3 %multiply_reduce_fusion = f32[256]{0:T(256)S(1)} fusion(bf16[256,1024]{1,0:T(8,128)(2,1)} %param.17, f32[256]{0:T(256)S(1)} %broadcast_multiply_fusion), kind=kLoop, calls=%fused_computation.20 | loop fusion | flops 1048320 | bytes 526336 | tf_op jit(solution)/shard_map/reduce_sum | solution.py:180
  3.4 0.0 copy-done
  3.4 0.0 copy-start.4
  3.4 0.0 copy-start.5
  3.4 6.3 %fusion.89 = (bf16[256,1024]{1,0:T(8,128)(2,1)S(1)}, f32[256,1024]{1,0:T(8,128)}) fusion(bf16[1024,1024]{1,0:T(8,128)(2,1)S(1)} %copy-done, bf16[1024,1024]{1,0:T(8,128)(2,1)} %param.21, bf16[256,1024]{1,0:T(8,128)(2,1)} %param.17, f32[1024]{0:T(1024)} %param.22, f32[1024]{0:T(1024)} %param.20, f32[1024]{0:T(1024)} %param.19, f32[256]{0:T(256)S(1)} %add_rsqrt_fusion, ...), kind=kOutput, calls=%fused_computation.120 | convolution fusion | flops 1092878336 | bytes 6305792 | tf_op jit(solution)/shard_map/dot_general | solution.py:188
  9.7 0.8 constant_dynamic-slice_fusion.1
  10.4 3.0 %collective-permute-start.4 = (bf16[256,256]{1,0:T(8,128)(2,1)}, bf16[256,256]{1,0:T(8,128)(2,1)}, u32[]{:S(2)}, u32[]{:S(2)}) collective-permute-start(bf16[256,256]{1,0:T(8,128)(2,1)} %get-tuple-element.31), channel_id=1, source_target_pairs={{0,1},{1,2},{2,3},{3,0},{4,5},{5,6},{6,7},{7,4},{8,9},{9,10},{10,1... | collective-permute-start | bytes 393224 | tf_op jit(solution)/shard_map/ppermute | solution.py:141
  13.5 2.0 %collective-permute-start.6 = (bf16[256,256]{1,0:T(8,128)(2,1)}, bf16[256,256]{1,0:T(8,128)(2,1)}, u32[]{:S(2)}, u32[]{:S(2)}) collective-permute-start(bf16[256,256]{1,0:T(8,128)(2,1)} %get-tuple-element.32), channel_id=1, source_target_pairs={{0,3},{1,0},{2,1},{3,2},{4,7},{5,4},{6,5},{7,6},{8,11},{9,8},{10,9... | collective-permute-start | bytes 393224 | tf_op jit(solution)/shard_map/ppermute | solution.py:141
  15.5 1.0 %collective-permute-start.5 = (bf16[256,256]{1,0:T(8,128)(2,1)}, bf16[256,256]{1,0:T(8,128)(2,1)}, u32[]{:S(2)}, u32[]{:S(2)}) collective-permute-start(bf16[256,256]{1,0:T(8,128)(2,1)} %get-tuple-element.33), channel_id=1, source_target_pairs={{0,2},{1,3},{2,0},{3,1},{4,6},{5,7},{6,4},{7,5},{8,10},{9,11},{10,... | collective-permute-start | bytes 393224 | tf_op jit(solution)/shard_map/ppermute | solution.py:141
  16.5 0.7 pad_maximum_fusion.right_ref
  17.3 7.5 %partial_kv.1 = (bf16[4,449,256]{2,1,0:T(8,128)(2,1)}, bf16[4,449,256]{2,1,0:T(8,128)(2,1)}) custom-call(s32[1]{0:T(128)} %bitcast.1.core_ref, bf16[512,3584]{1,0:T(8,128)(2,1)} %left_ref.1, bf16[512,256]{1,0:T(8,128)(2,1)} %pad_maximum_fusion.right_ref), custom_call_target="tpu_custom_call" | custom-call | tf_op jit(solution)/shard_map/partial_kv/pallas_call | solution.py:62
  24.7 1.6 %copy.22 = bf16[4,449,256]{2,0,1:T(4,128)(2,1)S(1)} copy(bf16[4,449,256]{2,1,0:T(8,128)(2,1)} %get-tuple-element.17) | data formatting | bytes 1839104 | tf_op jit(solution)/shard_map/partial_kv/pallas_call | solution.py:62
  26.3 0.1 collective-permute-start
  26.4 0.2 reduce-window.4
  26.6 0.5 copy-done.8
  27.1 0.6 slice.28
  27.7 0.7 fusion.55
  28.4 1.1 %convert_element_type.55 = f32[256,1024]{1,0:T(8,128)} convert(bf16[256,1024]{1,0:T(8,128)(2,1)S(1)} %copy-done.1) | non-fusion elementwise | flops 262144 | bytes 1572864 | tf_op jit(solution)/shard_map/convert_element_type | solution.py:178
  29.5 0.7 convert_reduce_fusion.1
  30.2 0.8 dynamic_slice.27
  31.0 0.8 dynamic_slice.22
  31.7 0.2 select_reduce_fusion.3
  31.9 0.1 select_reduce_fusion.2
  32.0 0.6 compare_select_fusion
  32.6 0.0 collective-permute-done.4
  32.7 0.0 collective-permute-done.6
  32.7 0.0 collective-permute-done.5
  32.7 1.5 %convolution_convert_fusion = bf16[256,256]{1,0:T(8,128)(2,1)S(1)} fusion(bf16[256,256]{1,0:T(8,128)(2,1)} %collective-permute-done.6, bf16[256,256]{1,0:T(8,128)(2,1)} %collective-permute-done.5, bf16[256,256]{1,0:T(8,128)(2,1)} %collective-permute-done.4, f32[256,1024]{1,0:T(8,128)} %get-tuple-element.43, s32[]{:T(128)S(6)} %select_n.52, ...), kind=kOutput, calls=%fused_computation.2 | convolution fusion | flops 34340864 | bytes 1051652 | tf_op jit(solution)/shard_map/dot_general | solution.py:162
  34.2 0.5 collective-permute-start.7
  34.7 1.5 %collective-permute-start.10 = (bf16[64,256]{1,0:T(8,128)(2,1)S(1)}, bf16[64,256]{1,0:T(8,128)(2,1)S(1)}, u32[]{:S(2)}, u32[]{:S(2)}) collective-permute-start(bf16[64,256]{1,0:T(8,128)(2,1)S(1)} %get-tuple-element.39), channel_id=1, source_target_pairs={{0,16},{4,20},{8,24},{12,28},{16,0},{20,4},{24,8},{28,12},{1,17},{... | collective-permute-start | bytes 98312 | tf_op jit(solution)/shard_map/ppermute | solution.py:141
  36.2 0.9 %collective-permute-start.9 = (bf16[64,256]{1,0:T(8,128)(2,1)S(1)}, bf16[64,256]{1,0:T(8,128)(2,1)S(1)}, u32[]{:S(2)}, u32[]{:S(2)}) collective-permute-start(bf16[64,256]{1,0:T(8,128)(2,1)S(1)} %get-tuple-element.40), channel_id=1, source_target_pairs={{0,12},{4,16},{8,20},{12,24},{16,28},{20,0},{24,4},{28,8},{1,13},{... | collective-permute-start | bytes 98312 | tf_op jit(solution)/shard_map/ppermute | solution.py:141
  37.1 1.5 %collective-permute-start.8 = (bf16[64,256]{1,0:T(8,128)(2,1)S(1)}, bf16[64,256]{1,0:T(8,128)(2,1)S(1)}, u32[]{:S(2)}, u32[]{:S(2)}) collective-permute-start(bf16[64,256]{1,0:T(8,128)(2,1)S(1)} %get-tuple-element.41), channel_id=1, source_target_pairs={{0,8},{4,12},{8,16},{12,20},{16,24},{20,28},{24,0},{28,4},{1,9},{5... | collective-permute-start | bytes 98312 | tf_op jit(solution)/shard_map/ppermute | solution.py:141
  38.6 0.0 collective-permute-done.7
  38.6 0.5 collective-permute-done.10
  39.1 0.4 collective-permute-done.9
  39.6 2.4 %collective-permute-done.8 = bf16[64,256]{1,0:T(8,128)(2,1)S(1)} collective-permute-done((bf16[64,256]{1,0:T(8,128)(2,1)S(1)}, bf16[64,256]{1,0:T(8,128)(2,1)S(1)}, u32[]{:S(2)}, u32[]{:S(2)}) %collective-permute-start.8) | collective-permute-done | bytes 32800 | tf_op jit(solution)/shard_map/ppermute | solution.py:141
  42.0 0.7 fusion.86
  42.7 6.7 %partial_proj.1 = (bf16[4,449,256]{2,1,0:T(8,128)(2,1)}, bf16[4,449,256]{2,1,0:T(8,128)(2,1)}) custom-call(s32[1]{0:T(128)} %bitcast.1.core_ref, bf16[256,3584]{1,0:T(8,128)(2,1)} %bitcast.23, bf16[256,256]{1,0:T(8,128)(2,1)} %bitcast.24), custom_call_target="tpu_custom_call" | custom-call | tf_op jit(solution)/shard_map/partial_proj/pallas_call | solution.py:62
  49.4 2.5 %copy.24 = bf16[4,449,256]{2,0,1:T(4,128)(2,1)} copy(bf16[4,449,256]{2,1,0:T(8,128)(2,1)} %get-tuple-element.23) | data formatting | bytes 1839104 | tf_op jit(solution)/shard_map/partial_proj/pallas_call | solution.py:62
  51.8 0.0 collective-permute-start.11
  51.8 0.0 collective-permute-done
  51.9 2.3 %copy.23.got_ref = bf16[4,449,256]{2,1,0:T(8,128)(2,1)} copy(bf16[4,449,256]{2,0,1:T(4,128)(2,1)} %collective-permute-done) | data formatting | bytes 1839104 | tf_op jit(solution)/shard_map/ppermute | solution.py:23
  54.1 2.6 %chip_kv.1 = (f32[449,256]{1,0:T(8,128)}, bf16[449,256]{1,0:T(8,128)(2,1)}, bf16[449,256]{1,0:T(8,128)(2,1)}, bf16[449,256]{1,0:T(8,128)(2,1)}) custom-call(s32[1]{0:T(128)} %bitcast.chip_ref, bf16[4,449,256]{2,1,0:T(8,128)(2,1)} %get-tuple-element.16.keep_ref, bf16[4,449,256]{2,1,0:T(8,128)(2,1)} %copy.23.got_ref), custom_call_target="tpu_custom_call" | custom-call | tf_op jit(solution)/shard_map/chip_kv/pallas_call | solution.py:93
  56.7 0.6 collective-permute-start.1
  57.3 1.5 %collective-permute-start.2 = (bf16[449,256]{1,0:T(8,128)(2,1)}, bf16[449,256]{1,0:T(8,128)(2,1)S(1)}, u32[]{:S(2)}, u32[]{:S(2)}) collective-permute-start(bf16[449,256]{1,0:T(8,128)(2,1)} %get-tuple-element.20), channel_id=1, source_target_pairs={{0,16},{4,20},{8,24},{12,28},{16,0},{20,4},{24,8},{28,12},{1,17},{... | collective-permute-start | bytes 689672 | tf_op jit(solution)/shard_map/ppermute | solution.py:18
  58.9 2.3 %collective-permute-start.3 = (bf16[449,256]{1,0:T(8,128)(2,1)}, bf16[449,256]{1,0:T(8,128)(2,1)S(1)}, u32[]{:S(2)}, u32[]{:S(2)}) collective-permute-start(bf16[449,256]{1,0:T(8,128)(2,1)} %get-tuple-element.21), channel_id=1, source_target_pairs={{0,24},{4,28},{8,0},{12,4},{16,8},{20,12},{24,16},{28,20},{1,25},{... | collective-permute-start | bytes 689672 | tf_op jit(solution)/shard_map/ppermute | solution.py:18
  61.2 0.0 collective-permute-done.11
  61.2 2.2 %copy.25.got_ref = bf16[4,449,256]{2,1,0:T(8,128)(2,1)} copy(bf16[4,449,256]{2,0,1:T(4,128)(2,1)} %collective-permute-done.11) | data formatting | bytes 1839104 | tf_op jit(solution)/shard_map/ppermute | solution.py:23
  63.4 2.6 %chip_proj.1 = (f32[449,256]{1,0:T(8,128)}, bf16[449,256]{1,0:T(8,128)(2,1)}, bf16[449,256]{1,0:T(8,128)(2,1)}, bf16[449,256]{1,0:T(8,128)(2,1)}) custom-call(s32[1]{0:T(128)} %bitcast.chip_ref, bf16[4,449,256]{2,1,0:T(8,128)(2,1)} %get-tuple-element.22.keep_ref, bf16[4,449,256]{2,1,0:T(8,128)(2,1)} %copy.25.got_ref), custom_call_target="tpu_custom_call" | custom-call | tf_op jit(solution)/shard_map/chip_proj/pallas_call | solution.py:93
  66.0 0.0 collective-permute-start.12
  66.0 0.6 collective-permute-start.13
  66.6 0.0 collective-permute-done.1
  66.6 2.9 %collective-permute-start.14 = (bf16[449,256]{1,0:T(8,128)(2,1)}, bf16[449,256]{1,0:T(8,128)(2,1)S(1)}, u32[]{:S(2)}, u32[]{:S(2)}) collective-permute-start(bf16[449,256]{1,0:T(8,128)(2,1)} %get-tuple-element.27), channel_id=1, source_target_pairs={{0,24},{4,28},{8,0},{12,4},{16,8},{20,12},{24,16},{28,20},{1,25},{... | collective-permute-start | bytes 689672 | tf_op jit(solution)/shard_map/ppermute | solution.py:18
  69.5 2.1 %collective-permute-done.2 = bf16[449,256]{1,0:T(8,128)(2,1)S(1)} collective-permute-done((bf16[449,256]{1,0:T(8,128)(2,1)}, bf16[449,256]{1,0:T(8,128)(2,1)S(1)}, u32[]{:S(2)}, u32[]{:S(2)}) %collective-permute-start.2) | collective-permute-done | bytes 229920 | tf_op jit(solution)/shard_map/ppermute | solution.py:18
  71.5 0.0 collective-permute-done.3
  71.5 0.0 copy-done.2
  71.5 0.1 convert_add_fusion.1
  71.7 0.8 fusion.87
  72.5 4.1 %collective-permute-done.12 = bf16[449,256]{1,0:T(8,128)(2,1)S(1)} collective-permute-done((bf16[449,256]{1,0:T(8,128)(2,1)}, bf16[449,256]{1,0:T(8,128)(2,1)S(1)}, u32[]{:S(2)}, u32[]{:S(2)}) %collective-permute-start.12) | collective-permute-done | bytes 229920 | tf_op jit(solution)/shard_map/ppermute | solution.py:18
  76.5 3.9 %collective-permute-done.13 = bf16[449,256]{1,0:T(8,128)(2,1)S(1)} collective-permute-done((bf16[449,256]{1,0:T(8,128)(2,1)}, bf16[449,256]{1,0:T(8,128)(2,1)S(1)}, u32[]{:S(2)}, u32[]{:S(2)}) %collective-permute-start.13) | collective-permute-done | bytes 229920 | tf_op jit(solution)/shard_map/ppermute | solution.py:18
  80.4 0.7 collective-permute-done.14
  81.1 0.9 %convert_add_fusion = f32[449,256]{1,0:T(8,128)} fusion(bf16[449,256]{1,0:T(8,128)(2,1)S(1)} %collective-permute-done.14, bf16[449,256]{1,0:T(8,128)(2,1)S(1)} %collective-permute-done.13, f32[449,256]{1,0:T(8,128)S(1)} %copy-done.3, bf16[449,256]{1,0:T(8,128)(2,1)S(1)} %collective-permute-done.12), kind=kLoop, calls=%fused_computation.60 | loop fusion | flops 689664 | bytes 1609216 | tf_op jit(solution)/shard_map/add | solution.py:113
  (15 shorter events, 0.0 us)
Async XLA Ops:
  0.6 2.8 %copy-start = (bf16[1024,1024]{1,0:T(8,128)(2,1)S(1)}, bf16[1024,1024]{1,0:T(8,128)(2,1)}, u32[]{:S(2)}) copy-start(bf16[1024,1024]{1,0:T(8,128)(2,1)} %param.23) | copy-start | bytes 6291460
  3.4 13.1 %copy-start.4 = (bf16[512,128]{1,0:T(8,128)(2,1)S(1)}, bf16[512,128]{1,0:T(8,128)(2,1)}, u32[]{:S(2)}) copy-start(bf16[512,128]{1,0:T(8,128)(2,1)} %param.16) | copy-start | bytes 393220
  3.4 13.1 %copy-start.5 = (bf16[512,128]{1,0:T(8,128)(2,1)S(1)}, bf16[512,128]{1,0:T(8,128)(2,1)}, u32[]{:S(2)}) copy-start(bf16[512,128]{1,0:T(8,128)(2,1)} %param.15) | copy-start | bytes 393220
  10.4 22.2 %collective-permute-start.4 = (bf16[256,256]{1,0:T(8,128)(2,1)}, bf16[256,256]{1,0:T(8,128)(2,1)}, u32[]{:S(2)}, u32[]{:S(2)}) collective-permute-start(bf16[256,256]{1,0:T(8,128)(2,1)} %get-tuple-element.31), channel_id=1, source_target_pairs={{0,1},{1,2},{2,3},{3,0},{4,5},{5,6},{6,7},{7,4},{8,9},{9,10},{10,1... | collective-permute-start | bytes 393224 | tf_op jit(solution)/shard_map/ppermute | solution.py:141
  13.5 19.2 %collective-permute-start.6 = (bf16[256,256]{1,0:T(8,128)(2,1)}, bf16[256,256]{1,0:T(8,128)(2,1)}, u32[]{:S(2)}, u32[]{:S(2)}) collective-permute-start(bf16[256,256]{1,0:T(8,128)(2,1)} %get-tuple-element.32), channel_id=1, source_target_pairs={{0,3},{1,0},{2,1},{3,2},{4,7},{5,4},{6,5},{7,6},{8,11},{9,8},{10,9... | collective-permute-start | bytes 393224 | tf_op jit(solution)/shard_map/ppermute | solution.py:141
  15.5 17.1 %collective-permute-start.5 = (bf16[256,256]{1,0:T(8,128)(2,1)}, bf16[256,256]{1,0:T(8,128)(2,1)}, u32[]{:S(2)}, u32[]{:S(2)}) collective-permute-start(bf16[256,256]{1,0:T(8,128)(2,1)} %get-tuple-element.33), channel_id=1, source_target_pairs={{0,2},{1,3},{2,0},{3,1},{4,6},{5,7},{6,4},{7,5},{8,10},{9,11},{10,... | collective-permute-start | bytes 393224 | tf_op jit(solution)/shard_map/ppermute | solution.py:141
  17.3 9.1 %copy-start.7 = (s32[1,8]{1,0:T(1,128)S(1)}, s32[1,8]{1,0:T(1,128)}, u32[]{:S(2)}) copy-start(s32[1,8]{1,0:T(1,128)} %param.26) | copy-start | bytes 100
  17.3 11.1 %copy-start.1 = (bf16[256,1024]{1,0:T(8,128)(2,1)S(1)}, bf16[256,1024]{1,0:T(8,128)(2,1)}, u32[]{:S(2)}) copy-start(bf16[256,1024]{1,0:T(8,128)(2,1)} %param.17) | copy-start | bytes 1572868
  24.7 7.0 %copy-start.6 = (s32[1,8]{1,0:T(1,128)S(1)}, s32[1,8]{1,0:T(1,128)}, u32[]{:S(2)}) copy-start(s32[1,8]{1,0:T(1,128)} %param.27) | copy-start | bytes 100
  26.3 25.6 %collective-permute-start = (bf16[4,449,256]{2,0,1:T(4,128)(2,1)S(1)}, bf16[4,449,256]{2,0,1:T(4,128)(2,1)}, u32[]{:S(2)}, u32[]{:S(2)}) collective-permute-start(bf16[4,449,256]{2,0,1:T(4,128)(2,1)S(1)} %copy.22), channel_id=1, source_target_pairs={{0,4},{4,0},{8,12},{12,8},{16,20},{20,16},{24,28},{28,24},{1,5},{5... | collective-permute-start | bytes 2758664 | tf_op jit(solution)/shard_map/ppermute | solution.py:23
  26.6 0.5 copy-start.8
  34.2 4.5 %collective-permute-start.7 = (bf16[64,256]{1,0:T(8,128)(2,1)S(1)}, bf16[64,256]{1,0:T(8,128)(2,1)S(1)}, u32[]{:S(2)}, u32[]{:S(2)}) collective-permute-start(bf16[64,256]{1,0:T(8,128)(2,1)S(1)} %get-tuple-element.38), channel_id=1, source_target_pairs={{0,4},{4,8},{8,12},{12,16},{16,20},{20,24},{24,28},{28,0},{1,5},{5... | collective-permute-start | bytes 98312 | tf_op jit(solution)/shard_map/ppermute | solution.py:141
  34.7 4.4 %collective-permute-start.10 = (bf16[64,256]{1,0:T(8,128)(2,1)S(1)}, bf16[64,256]{1,0:T(8,128)(2,1)S(1)}, u32[]{:S(2)}, u32[]{:S(2)}) collective-permute-start(bf16[64,256]{1,0:T(8,128)(2,1)S(1)} %get-tuple-element.39), channel_id=1, source_target_pairs={{0,16},{4,20},{8,24},{12,28},{16,0},{20,4},{24,8},{28,12},{1,17},{... | collective-permute-start | bytes 98312 | tf_op jit(solution)/shard_map/ppermute | solution.py:141
  36.2 3.3 %collective-permute-start.9 = (bf16[64,256]{1,0:T(8,128)(2,1)S(1)}, bf16[64,256]{1,0:T(8,128)(2,1)S(1)}, u32[]{:S(2)}, u32[]{:S(2)}) collective-permute-start(bf16[64,256]{1,0:T(8,128)(2,1)S(1)} %get-tuple-element.40), channel_id=1, source_target_pairs={{0,12},{4,16},{8,20},{12,24},{16,28},{20,0},{24,4},{28,8},{1,13},{... | collective-permute-start | bytes 98312 | tf_op jit(solution)/shard_map/ppermute | solution.py:141
  37.1 4.8 %collective-permute-start.8 = (bf16[64,256]{1,0:T(8,128)(2,1)S(1)}, bf16[64,256]{1,0:T(8,128)(2,1)S(1)}, u32[]{:S(2)}, u32[]{:S(2)}) collective-permute-start(bf16[64,256]{1,0:T(8,128)(2,1)S(1)} %get-tuple-element.41), channel_id=1, source_target_pairs={{0,8},{4,12},{8,16},{12,20},{16,24},{20,28},{24,0},{28,4},{1,9},{5... | collective-permute-start | bytes 98312 | tf_op jit(solution)/shard_map/ppermute | solution.py:141
  51.8 9.3 %collective-permute-start.11 = (bf16[4,449,256]{2,0,1:T(4,128)(2,1)}, bf16[4,449,256]{2,0,1:T(4,128)(2,1)}, u32[]{:S(2)}, u32[]{:S(2)}) collective-permute-start(bf16[4,449,256]{2,0,1:T(4,128)(2,1)} %copy.24), channel_id=1, source_target_pairs={{0,4},{4,0},{8,12},{12,8},{16,20},{20,16},{24,28},{28,24},{1,5},{5... | collective-permute-start | bytes 2758664 | tf_op jit(solution)/shard_map/ppermute | solution.py:23
  56.7 14.8 %copy-start.2 = (f32[449,256]{1,0:T(8,128)S(1)}, f32[449,256]{1,0:T(8,128)}, u32[]{:S(2)}) copy-start(f32[449,256]{1,0:T(8,128)} %get-tuple-element.18) | copy-start | bytes 1379332
  56.7 9.9 %collective-permute-start.1 = (bf16[449,256]{1,0:T(8,128)(2,1)}, bf16[449,256]{1,0:T(8,128)(2,1)S(1)}, u32[]{:S(2)}, u32[]{:S(2)}) collective-permute-start(bf16[449,256]{1,0:T(8,128)(2,1)} %get-tuple-element.19), channel_id=1, source_target_pairs={{0,8},{4,12},{8,16},{12,20},{16,24},{20,28},{24,0},{28,4},{1,9},{5... | collective-permute-start | bytes 689672 | tf_op jit(solution)/shard_map/ppermute | solution.py:18
  57.3 14.2 %collective-permute-start.2 = (bf16[449,256]{1,0:T(8,128)(2,1)}, bf16[449,256]{1,0:T(8,128)(2,1)S(1)}, u32[]{:S(2)}, u32[]{:S(2)}) collective-permute-start(bf16[449,256]{1,0:T(8,128)(2,1)} %get-tuple-element.20), channel_id=1, source_target_pairs={{0,16},{4,20},{8,24},{12,28},{16,0},{20,4},{24,8},{28,12},{1,17},{... | collective-permute-start | bytes 689672 | tf_op jit(solution)/shard_map/ppermute | solution.py:18
  58.9 12.7 %collective-permute-start.3 = (bf16[449,256]{1,0:T(8,128)(2,1)}, bf16[449,256]{1,0:T(8,128)(2,1)S(1)}, u32[]{:S(2)}, u32[]{:S(2)}) collective-permute-start(bf16[449,256]{1,0:T(8,128)(2,1)} %get-tuple-element.21), channel_id=1, source_target_pairs={{0,24},{4,28},{8,0},{12,4},{16,8},{20,12},{24,16},{28,20},{1,25},{... | collective-permute-start | bytes 689672 | tf_op jit(solution)/shard_map/ppermute | solution.py:18
  66.0 15.1 %copy-start.3 = (f32[449,256]{1,0:T(8,128)S(1)}, f32[449,256]{1,0:T(8,128)}, u32[]{:S(2)}) copy-start(f32[449,256]{1,0:T(8,128)} %get-tuple-element.24) | copy-start | bytes 1379332
  66.0 10.5 %collective-permute-start.12 = (bf16[449,256]{1,0:T(8,128)(2,1)}, bf16[449,256]{1,0:T(8,128)(2,1)S(1)}, u32[]{:S(2)}, u32[]{:S(2)}) collective-permute-start(bf16[449,256]{1,0:T(8,128)(2,1)} %get-tuple-element.25), channel_id=1, source_target_pairs={{0,8},{4,12},{8,16},{12,20},{16,24},{20,28},{24,0},{28,4},{1,9},{5... | collective-permute-start | bytes 689672 | tf_op jit(solution)/shard_map/ppermute | solution.py:18
  66.0 14.3 %collective-permute-start.13 = (bf16[449,256]{1,0:T(8,128)(2,1)}, bf16[449,256]{1,0:T(8,128)(2,1)S(1)}, u32[]{:S(2)}, u32[]{:S(2)}) collective-permute-start(bf16[449,256]{1,0:T(8,128)(2,1)} %get-tuple-element.26), channel_id=1, source_target_pairs={{0,16},{4,20},{8,24},{12,28},{16,0},{20,4},{24,8},{28,12},{1,17},{... | collective-permute-start | bytes 689672 | tf_op jit(solution)/shard_map/ppermute | solution.py:18
  66.6 14.5 %collective-permute-start.14 = (bf16[449,256]{1,0:T(8,128)(2,1)}, bf16[449,256]{1,0:T(8,128)(2,1)S(1)}, u32[]{:S(2)}, u32[]{:S(2)}) collective-permute-start(bf16[449,256]{1,0:T(8,128)(2,1)} %get-tuple-element.27), channel_id=1, source_target_pairs={{0,24},{4,28},{8,0},{12,4},{16,8},{20,12},{24,16},{28,20},{1,25},{... | collective-permute-start | bytes 689672 | tf_op jit(solution)/shard_map/ppermute | solution.py:18

commit v2 on v0

v2 whole, which is shorter than its diff:
```python
from functools import partial

import jax
import jax.numpy as jnp
from jax import lax
from jax.experimental import pallas as pl
from jax.experimental.pallas import tpu as pltpu
from jax.sharding import PartitionSpec as P

FEW = 8
CHUNK = 512
ANY = pl.BlockSpec(memory_space=pl.ANY)
VMEM = pl.BlockSpec(memory_space=pltpu.VMEM)
SMEM = pl.BlockSpec(memory_space=pltpu.SMEM)


def shifted(x, axis, by):
    count = lax.axis_size(axis)
    return lax.ppermute(x, axis, [(i, (i + by) % count) for i in range(count)])


def core_swap(x):
    count = lax.axis_size("dp")
    return lax.ppermute(x, "dp", [(i, i ^ 1) for i in range(count)])


def scalar(value):
    return jnp.reshape(value, (1,)).astype(jnp.int32)


def padded(rows):
    return (rows + 15) // 16 * 16


def partial_kernel(core_ref, left_hbm, *refs, parts, ranks, rows, ones_row):
    rights = refs[:parts]
    keep_hbm, send_hbm, left, right_ref, total, stage, in_sem, out_sem = refs[parts:]
    chunks, tokens, chunk = left.shape
    width = chunks * chunk
    stride = stage.shape[1]
    incoming = [
        pltpu.make_async_copy(left_hbm.at[:, pl.ds(c * chunk, chunk)], left.at[c], in_sem.at[c])
        for c in range(chunks)
    ]
    for copy in incoming:
        copy.start()
    if ones_row:
        right = jnp.concatenate([part[...] for part in rights], axis=1)
    else:
        right = jnp.concatenate([part[...] for part in rights], axis=0)
    right_ref[...] = right
    extra = total.shape[0] - width
    if ones_row:
        first = lax.broadcasted_iota(jnp.int32, (extra, tokens), 0) == 0
        picked = jnp.where(first, 1.0, 0.0).astype(jnp.bfloat16)
        total[width:, :] = jnp.dot(picked, right_ref[...], preferred_element_type=jnp.float32)
    else:
        total[width:, :] = jnp.zeros((extra, total.shape[1]), jnp.float32)
    tail = rows // 16 * 16
    if tail < rows:
        for rank in range(ranks):
            stage[rank, tail:, :] = jnp.zeros((stride - tail, total.shape[1]), jnp.bfloat16)

    def outgoing(rank, target):
        place = pl.ds(rank // 2 * stride, stride)
        return pltpu.make_async_copy(stage.at[rank], target.at[place, :], out_sem.at[rank])

    rank = 0
    for c in range(chunks):
        incoming[c].wait()
        total[c * chunk : (c + 1) * chunk, :] = lax.dot_general(
            left[c], right_ref[...], (((0,), (0,)), ((), ())), preferred_element_type=jnp.float32
        )
        ready = (c + 1) * chunk if c + 1 < chunks else ranks * rows
        while rank < ranks and (rank + 1) * rows <= ready:
            stage[rank, :rows, :] = total[rank * rows : (rank + 1) * rows, :].astype(jnp.bfloat16)

            @pl.when(core_ref[0] == rank % 2)
            def _(rank=rank):
                outgoing(rank, keep_hbm).start()

            @pl.when(core_ref[0] != rank % 2)
            def _(rank=rank):
                outgoing(rank, send_hbm).start()

            rank += 1
    for rank in range(ranks):
        outgoing(rank, keep_hbm).wait()


def partial_blocks(left, rights, ranks, rows, ones_row):
    tokens, width = left.shape
    cols = sum(part.shape[1] for part in rights) if ones_row else rights[0].shape[1]
    chunk = CHUNK if width % CHUNK == 0 else width
    stride = padded(rows)
    block = jax.ShapeDtypeStruct((ranks // 2 * stride, cols), jnp.bfloat16)
    return pl.pallas_call(
        partial(partial_kernel, parts=len(rights), ranks=ranks, rows=rows, ones_row=ones_row),
        out_shape=(block, block),
        in_specs=[SMEM, ANY] + [VMEM] * len(rights),
        out_specs=(ANY, ANY),
        scratch_shapes=[
            pltpu.VMEM((width // chunk, tokens, chunk), jnp.bfloat16),
            pltpu.VMEM((tokens, cols), jnp.bfloat16),
            pltpu.VMEM((ranks * rows, cols), jnp.float32),
            pltpu.VMEM((ranks, stride, cols), jnp.bfloat16),
            pltpu.SemaphoreType.DMA((width // chunk,)),
            pltpu.SemaphoreType.DMA((ranks,)),
        ],
        name="partial_kv" if ones_row else "partial_proj",
    )(scalar(lax.axis_index("dp") % 2), left, *rights)


def chip_sum_kernel(chip_ref, keep_hbm, got_hbm, *refs):
    chips = (len(refs) - 5) if len(refs) > 5 else 1
    outs = refs[:chips]
    keep, got, stage, in_sem, out_sem = refs[chips:]
    stride = keep.shape[1]
    rows = outs[0].shape[0]
    order = list(range(1, chips)) + [0]
    copies = {}
    for distance in order:
        target = lax.rem(chip_ref[0] + distance, chips)
        place = pl.ds(pl.multiple_of(target * stride, 16), stride)
        copies[distance] = (
            pltpu.make_async_copy(keep_hbm.at[place, :], keep.at[distance], in_sem.at[distance, 0]),
            pltpu.make_async_copy(got_hbm.at[place, :], got.at[distance], in_sem.at[distance, 1]),
        )
        for copy in copies[distance]:
            copy.start()
    leaving = []
    for distance in order:
        for copy in copies[distance]:
            copy.wait()
        total = keep[distance].astype(jnp.float32) + got[distance].astype(jnp.float32)
        if distance == 0:
            outs[0][...] = total[:rows, :]
        else:
            stage[distance - 1] = total.astype(jnp.bfloat16)
            leaving.append(
                pltpu.make_async_copy(stage.at[distance - 1], outs[distance], out_sem.at[distance - 1])
            )
            leaving[-1].start()
    for copy in leaving:
        copy.wait()


def chip_sums(keep, got, chips, rows, name):
    stride, cols = keep.shape[0] // chips, keep.shape[1]
    return pl.pallas_call(
        chip_sum_kernel,
        in_specs=[SMEM, ANY, ANY],
        out_specs=(VMEM,) + (ANY,) * (chips - 1),
        out_shape=(jax.ShapeDtypeStruct((rows, cols), jnp.float32),)
        + (jax.ShapeDtypeStruct((stride, cols), jnp.bfloat16),) * (chips - 1),
        scratch_shapes=[
            pltpu.VMEM((chips, stride, cols), jnp.bfloat16),
            pltpu.VMEM((chips, stride, cols), jnp.bfloat16),
            pltpu.VMEM((max(chips - 1, 1), stride, cols), jnp.bfloat16),
            pltpu.SemaphoreType.DMA((chips, 2)),
            pltpu.SemaphoreType.DMA((max(chips - 1, 1),)),
        ],
        name=name,
    )(scalar(lax.axis_index("dp") // 2), keep, got)


def spread_sums(own, sends):
    rows = own.shape[0]
    total = own
    for distance, block in enumerate(sends, 1):
        total = total + shifted(block, "dp", 2 * distance)[:rows].astype(jnp.float32)
    return total


def plain_rows(left, right, ranks, rows, ones_row):
    tokens, width = left.shape
    filler = jnp.zeros((tokens, ranks * rows - width), jnp.bfloat16)
    if ones_row:
        filler = filler.at[:, 0].set(1)
    wide = jnp.concatenate([left, filler], axis=1)
    product = lax.dot_general(wide, right, (((0,), (0,)), ((), ())), preferred_element_type=jnp.float32)
    return lax.psum_scatter(product, "dp", scatter_dimension=0, tiled=True)


def encoder_kernel(me_ref, rows_ref, gain_ref, bias_ref, fc1_ref, b1_ref, fc2_ref, own_ref, *refs):
    sends = refs[:-2]
    normed, total = refs[-2:]
    shards, _, cols = total.shape
    step = pl.program_id(0)

    @pl.when(step == 0)
    def _():
        values = rows_ref[...].astype(jnp.float32)
        center = jnp.mean(values, axis=1, keepdims=True)
        moved = values - center
        spread_sq = jnp.mean(moved * moved, axis=1, keepdims=True)
        normed[...] = (moved * lax.rsqrt(spread_sq + 1e-06) * gain_ref[...] + bias_ref[...]).astype(
            jnp.bfloat16
        )

    before = jnp.dot(normed[...], fc1_ref[...], preferred_element_type=jnp.float32) + b1_ref[...]
    hidden = (0.5 * before * (1.0 + lax.erf(before * 0.7071067811865476))).astype(jnp.bfloat16)
    for shard in range(shards):
        piece = jnp.dot(
            hidden, fc2_ref[:, shard * cols : (shard + 1) * cols], preferred_element_type=jnp.float32
        )

        @pl.when(step == 0)
        def _(piece=piece, shard=shard):
            total[shard] = piece

        @pl.when(step > 0)
        def _(piece=piece, shard=shard):
            total[shard] += piece

    @pl.when(step == pl.num_programs(0) - 1)
    def _():
        own_ref[...] = total[me_ref[0]]
        for distance, send in enumerate(sends, 1):
            send[...] = total[lax.rem(me_ref[0] + distance, shards)].astype(jnp.bfloat16)


def encoder_partials(rows, gain, bias, fc1, b1, fc2):
    shards = lax.axis_size("mp")
    count, feats = rows.shape
    units = fc1.shape[1]
    chunk = 256 if units % 256 == 0 else units
    cols = feats // shards
    block = pl.BlockSpec((count, cols), lambda i, m: (0, 0))
    line = pl.BlockSpec((1, feats), lambda i, m: (0, 0))
    return pl.pallas_call(
        encoder_kernel,
        out_shape=(jax.ShapeDtypeStruct((count, cols), jnp.float32),)
        + (jax.ShapeDtypeStruct((count, cols), jnp.bfloat16),) * (shards - 1),
        grid_spec=pltpu.PrefetchScalarGridSpec(
            num_scalar_prefetch=1,
            grid=(units // chunk,),
            in_specs=[
                pl.BlockSpec((count, feats), lambda i, m: (0, 0)),
                line,
                line,
                pl.BlockSpec((feats, chunk), lambda i, m: (0, i)),
                pl.BlockSpec((1, chunk), lambda i, m: (0, i)),
                pl.BlockSpec((chunk, feats), lambda i, m: (i, 0)),
            ],
            out_specs=(block,) * shards,
            scratch_shapes=[
                pltpu.VMEM((count, feats), jnp.bfloat16),
                pltpu.VMEM((shards, count, cols), jnp.float32),
            ],
        ),
        name="encoder",
    )(scalar(lax.axis_index("mp")), rows, gain[None], bias[None], fc1, b1[None], fc2)


def pack_kernel(me_ref, counts_ref, offsets_ref, rows_ref, scale_ref, bias_ref, own_ref, *refs, spread):
    parts, outs = refs[:-spread], refs[-spread:]
    images = counts_ref.shape[0]
    cap = outs[0].shape[0]
    total_rows = rows_ref.shape[0]
    summed = own_ref[...]
    for part in parts:
        summed = summed + part[...].astype(jnp.float32)
    encoded = rows_ref[...].astype(jnp.float32) + scale_ref[...] * (summed + bias_ref[...])
    encoded = encoded.astype(jnp.bfloat16)
    place = lax.broadcasted_iota(jnp.int32, (1, total_rows), 1)
    target = jnp.full((1, total_rows), -1, jnp.int32)
    start = jnp.int32(0)
    for image in range(images):
        count, offset = counts_ref[image], offsets_ref[image]
        before = jnp.int32(0)
        for other in range(image):
            before = before + jnp.where(offsets_ref[other] == offset, counts_ref[other], 0)
        inside = (place >= start) & (place < start + count)
        target = jnp.where(inside, place + ((offset - 1) * cap + before - start), target)
        start = start + count
    slot = lax.broadcasted_iota(jnp.int32, (spread * cap, total_rows), 0)
    select = jnp.where(slot == target, 1.0, 0.0).astype(jnp.bfloat16)
    packed = jnp.dot(select, encoded, preferred_element_type=jnp.float32).astype(jnp.bfloat16)
    for distance in range(spread):
        outs[distance][...] = packed[distance * cap : (distance + 1) * cap, :]


def packed_rows(rows, scale, bias, own, parts, counts, offsets, spread, cap):
    count, cols = own.shape
    line = pl.BlockSpec((1, cols), lambda i, m, c, o: (0, m[0]))
    whole = pl.BlockSpec((count, cols), lambda i, m, c, o: (0, 0))
    return pl.pallas_call(
        partial(pack_kernel, spread=spread),
        out_shape=(jax.ShapeDtypeStruct((cap, cols), jnp.bfloat16),) * spread,
        grid_spec=pltpu.PrefetchScalarGridSpec(
            num_scalar_prefetch=3,
            grid=(1,),
            in_specs=[pl.BlockSpec((count, cols), lambda i, m, c, o: (0, m[0])), line, line]
            + [whole] * (1 + len(parts)),
            out_specs=(pl.BlockSpec((cap, cols), lambda i, m, c, o: (0, 0)),) * spread,
        ),
        name="pack",
    )(scalar(lax.axis_index("mp")), counts, offsets, rows, scale[None], bias[None], own, *parts)


def per_device(
    hidden_rows,
    key_grad,
    value_grad,
    visual_rows,
    visual_cotangent,
    norm_gain,
    norm_bias,
    fc1_weight,
    fc1_bias,
    fc2_weight,
    fc2_bias,
    layer_scale,
    token_counts,
    dest_offsets,
):
    width = hidden_rows.shape[1]
    ranks = lax.axis_size("dp")
    rows = (width + ranks) // ranks
    spread, cap = visual_cotangent.shape[1:3]
    key_cols = key_grad.shape[1]
    stepped = ranks <= FEW and ranks % 2 == 0
    chips = ranks // 2

    own, *sends = encoder_partials(
        visual_rows, norm_gain, norm_bias, fc1_weight, fc1_bias, fc2_weight
    )
    parts = [shifted(block, "mp", distance) for distance, block in enumerate(sends, 1)]
    if stepped:
        left, own = lax.optimization_barrier((hidden_rows, own))
        kv_keep, kv_send = partial_blocks(left, (key_grad, value_grad), ranks, rows, True)
        kv_got = core_swap(kv_send)
        own, kv_keep = lax.optimization_barrier((own, kv_keep))
    packed = packed_rows(
        visual_rows,
        layer_scale,
        fc2_bias,
        own,
        parts,
        token_counts[0],
        dest_offsets[0],
        spread,
        cap,
    )
    if stepped:
        packed, kv_keep = lax.optimization_barrier((packed, kv_keep))
    received = [shifted(block, "dp", distance) for distance, block in enumerate(packed, 1)]
    handoff = jnp.stack(received, axis=0)[None]
    cotangent = visual_cotangent.reshape(spread * cap, width)
    if stepped:
        kv_own, *kv_sends = chip_sums(kv_keep, kv_got, chips, rows, "chip_kv")
        cotangent, kv_own = lax.optimization_barrier((cotangent, kv_own))
        keep, send = partial_blocks(cotangent, received, ranks, rows, False)
        got = core_swap(send)
        kv_results = spread_sums(kv_own, kv_sends)
        proj_own, *proj_sends = chip_sums(keep, got, chips, rows, "chip_proj")
        projector_grad = spread_sums(proj_own, proj_sends)
    else:
        kv_cotangent = jnp.concatenate([key_grad, value_grad], axis=1)
        kv_results = plain_rows(hidden_rows, kv_cotangent, ranks, rows, True)
        projector_grad = plain_rows(
            cotangent, handoff.reshape(spread * cap, handoff.shape[3]), ranks, rows, False
        )
    return (kv_results[:, :key_cols], kv_results[:, key_cols:], projector_grad, handoff)


def solution(mesh):
    placed = (
        P("dp", None),
        P("dp", "mp"),
        P("dp", "mp"),
        P("dp", None),
        P("dp", None, None, None),
        P(),
        P(),
        P(None, "mp"),
        P("mp"),
        P("mp", None),
        P(),
        P(),
        P("dp", None),
        P("dp", None),
    )
    return jax.shard_map(
        per_device,
        mesh=mesh,
        in_specs=placed,
        out_specs=(P("dp", "mp"), P("dp", "mp"), P("dp", "mp"), P("dp", None, None, "mp")),
        check_vma=False,
    )
```

time: 159 us -> 82.5 us (0.52)
  blocking collectives: 57.2 us -> 0 us
  Pallas kernels: 0 us -> 27.4 us
  waiting for transfers between devices: 43.2 us -> 25.7 us
  matrix products: 17.1 us -> 0 us
  between operations: 17 us -> 0.81 us
  starting transfers between devices: 4.79 us -> 19.8 us
  local copies, waits for them, and re-layouts: 13.3 us -> 4.57 us
  other arithmetic: 5.67 us -> 3.52 us
    unnamed x1 -> x0, blocking collectives: 57.2 us -> none
    pallas_call x0 -> x6, Pallas kernels: none -> 27.4 us  [the longest x2 10.6 us: partial_blocks(): pl.pallas_call(partial(partial_kernel, parts=len(rights), ranks=ranks, ro...]
    ppermute x4 -> x13, waiting for transfers between devices: 0.01 us -> 25.7 us  [shifted(): return lax.ppermute(x, axis, [(i, (i + by) % count) for i in range(count)])]
    unnamed x4 -> x0, waiting for transfers between devices: 24.3 us -> none
    reduce_scatter x1 -> x0, waiting for transfers between devices: 18.9 us -> none  [vision(): lax.psum_scatter(partial_value, 'mp', scatter_dimension=1, tiled=True)]
    dot_general x4 -> x0, matrix products: 17.1 us -> none  [the longest x1 6.29 us: vision(): jnp.dot(hidden, fc2_weight, preferred_element_type=jnp.float32)]
    ppermute x4 -> x13, starting transfers between devices: 3.41 us -> 19.2 us  [shifted(): return lax.ppermute(x, axis, [(i, (i + by) % count) for i in range(count)])]
    concatenate x1 -> x0, local copies, waits for them, and re-layouts: 6.67 us -> none  [per_device(): jnp.concatenate([hidden_rows, ones_column, zero_columns], axis=1)]
  transfers between devices with their start and end apart: 7 -> 15, of which waited for: 2 -> 7; matrix products, arithmetic and copies ran while one was open for 51% -> 3% of each run, Pallas kernels for 0% -> 7%
where the time goes in v2:
time: 82.5 us; the launch traced here: 81.8 us
  Pallas kernels  27.4 us (33%)
  waiting for transfers between devices  25.7 us (31%)
  starting transfers between devices  19.8 us (24%)
  local copies, waits for them, and re-layouts  4.57 us (6%)
  other arithmetic  3.52 us (4%)
    ppermute x13, waiting for transfers between devices, shifted(): return lax.ppermute(x, axis, [(i, (i + by) % count) for i in range(count)])  25.7 us
    ppermute x13, starting transfers between devices, shifted(): return lax.ppermute(x, axis, [(i, (i + by) % count) for i in range(count)])  19.2 us
    pallas_call x2, Pallas kernels, partial_blocks(): pl.pallas_call(partial(partial_kernel, parts=len(rights), ranks=ranks, ro...  10.6 us
    pallas_call x1, Pallas kernels, encoder_partials(): pl.pallas_call(encoder_kernel, out_shape=(jax.ShapeDtypeStruct((count, co...  7.89 us
    pallas_call x2, Pallas kernels, chip_sums(): pl.pallas_call(chip_sum_kernel, in_specs=[SMEM, ANY, ANY], out_specs=(VME...  6.12 us
    unnamed x26, local copies, waits for them, and re-layouts  3.78 us
    pallas_call x1, Pallas kernels, packed_rows(): pl.pallas_call(partial(pack_kernel, spread=spread), out_shape=(jax.ShapeD...  2.75 us
    add x2, other arithmetic, spread_sums(): total + shifted(block, 'dp', 2 * distance)[:rows].astype(jnp.float32)  2.04 us
  transfers between devices with their start and end apart: 15, of which 7 were waited for; matrix products, arithmetic and copies ran while one was open for 3% of the time, Pallas kernels for 7%

profile of v2, /device:TPU:0, one launch (start us, length us, event | category | flops | bytes accessed | tf_op | source)
XLA Modules:
  0.0 81.8 jit_solution(2879612124578219897)
XLA Ops:
  0.6 7.9 %encoder.1 = (f32[256,256]{1,0:T(8,128)}, bf16[256,256]{1,0:T(8,128)(2,1)}, bf16[256,256]{1,0:T(8,128)(2,1)}, bf16[256,256]{1,0:T(8,128)(2,1)}) custom-call(s32[1]{0:T(128)} %bitcast.2.me_ref, bf16[256,1024]{1,0:T(8,128)(2,1)} %rows_ref.3, f32[1,1024]{1,0:T(1,128)} %bitcast.24, f32[1,1024]{1,0:T(1,128)} %bitcast.25, bf16[1024,1024]{1,0:T(8,128)(2,1)} %fc1_ref.1, ...), custom_call_target="tpu_custom_call" | custom-call | tf_op jit(solution)/shard_map/encoder/pallas_call | solution.py:231
  8.5 0.0 copy-start.12
  8.5 0.0 copy-start.11
  8.5 0.0 copy-start.10
  8.6 5.9 %partial_kv.1 = (bf16[1856,256]{1,0:T(8,128)(2,1)}, bf16[1856,256]{1,0:T(8,128)(2,1)}) custom-call(s32[1]{0:T(128)} %bitcast.10.core_ref, bf16[512,3584]{1,0:T(8,128)(2,1)} %left_hbm, bf16[512,128]{1,0:T(8,128)(2,1)} %refs_0_.1, bf16[512,128]{1,0:T(8,128)(2,1)} %refs_1_.1), custom_call_target="tpu_custom_call" | custom-call | tf_op jit(solution)/shard_map/partial_kv/pallas_call | solution.py:97
  14.5 0.6 collective-permute-start.3
  15.1 0.0 copy-done.12
  15.1 2.6 %collective-permute-start = (bf16[256,256]{1,0:T(8,128)(2,1)S(1)}, bf16[256,256]{1,0:T(8,128)(2,1)S(1)}, u32[]{:S(2)}, u32[]{:S(2)}) collective-permute-start(bf16[256,256]{1,0:T(8,128)(2,1)S(1)} %copy-done.12), channel_id=1, source_target_pairs={{0,1},{1,2},{2,3},{3,0},{4,5},{5,6},{6,7},{7,4},{8,9},{9,10},{10,1... | collective-permute-start | bytes 393224 | tf_op jit(solution)/shard_map/ppermute | solution.py:19
  17.7 0.0 copy-done.11
  17.7 2.6 %collective-permute-start.1 = (bf16[256,256]{1,0:T(8,128)(2,1)S(1)}, bf16[256,256]{1,0:T(8,128)(2,1)S(1)}, u32[]{:S(2)}, u32[]{:S(2)}) collective-permute-start(bf16[256,256]{1,0:T(8,128)(2,1)S(1)} %copy-done.11), channel_id=1, source_target_pairs={{0,2},{1,3},{2,0},{3,1},{4,6},{5,7},{6,4},{7,5},{8,10},{9,11},{10,... | collective-permute-start | bytes 393224 | tf_op jit(solution)/shard_map/ppermute | solution.py:19
  20.3 0.0 copy-done.10
  20.3 1.3 %collective-permute-start.2 = (bf16[256,256]{1,0:T(8,128)(2,1)S(1)}, bf16[256,256]{1,0:T(8,128)(2,1)S(1)}, u32[]{:S(2)}, u32[]{:S(2)}) collective-permute-start(bf16[256,256]{1,0:T(8,128)(2,1)S(1)} %copy-done.10), channel_id=1, source_target_pairs={{0,3},{1,0},{2,1},{3,2},{4,7},{5,4},{6,5},{7,6},{8,11},{9,8},{10,9... | collective-permute-start | bytes 393224 | tf_op jit(solution)/shard_map/ppermute | solution.py:19
  21.6 2.5 %collective-permute-done.refs_0_ = bf16[256,256]{1,0:T(8,128)(2,1)S(1)} collective-permute-done((bf16[256,256]{1,0:T(8,128)(2,1)S(1)}, bf16[256,256]{1,0:T(8,128)(2,1)S(1)}, u32[]{:S(2)}, u32[]{:S(2)}) %collective-permute-start) | collective-permute-done | bytes 131104 | tf_op jit(solution)/shard_map/ppermute | solution.py:19
  24.2 0.0 copy-start.7
  24.2 5.3 %collective-permute-done.1.refs_1_ = bf16[256,256]{1,0:T(8,128)(2,1)S(1)} collective-permute-done((bf16[256,256]{1,0:T(8,128)(2,1)S(1)}, bf16[256,256]{1,0:T(8,128)(2,1)S(1)}, u32[]{:S(2)}, u32[]{:S(2)}) %collective-permute-start.1) | collective-permute-done | bytes 131104 | tf_op jit(solution)/shard_map/ppermute | solution.py:19
  29.5 0.0 copy-start.8
  29.5 0.0 collective-permute-done.2.refs_2_
  29.5 0.0 copy-start.9
  29.5 0.0 copy-done.7
  29.5 0.6 copy-done.8
  30.2 0.0 copy-done.9
  30.2 2.8 %pack.1 = (bf16[64,256]{1,0:T(8,128)(2,1)}, bf16[64,256]{1,0:T(8,128)(2,1)}, bf16[64,256]{1,0:T(8,128)(2,1)}, bf16[64,256]{1,0:T(8,128)(2,1)}) custom-call(s32[1]{0:T(128)} %bitcast.2.me_ref, s32[8]{0:T(128)} %bitcast.27, s32[8]{0:T(128)} %bitcast.28, bf16[256,1024]{1,0:T(8,128)(2,1)} %rows_ref.3, f32[1,1024]{1,0:T(1,128)} %bitcast.22, f32[1,1024]{1,0:T(1,128)} %bitcast.23, ...), custom_call_target="tpu_custom_call" | custom-call | tf_op jit(solution)/shard_map/pack/pallas_call | solution.py:288
  33.0 0.0 collective-permute-start.7
  33.0 1.5 %collective-permute-start.8 = (bf16[64,256]{1,0:T(8,128)(2,1)}, bf16[64,256]{1,0:T(8,128)(2,1)S(1)}, u32[]{:S(2)}, u32[]{:S(2)}) collective-permute-start(bf16[64,256]{1,0:T(8,128)(2,1)} %get-tuple-element.57), channel_id=1, source_target_pairs={{0,8},{4,12},{8,16},{12,20},{16,24},{20,28},{24,0},{28,4},{1,9},{5... | collective-permute-start | bytes 98312 | tf_op jit(solution)/shard_map/ppermute | solution.py:19
  34.5 2.4 %collective-permute-start.9 = (bf16[64,256]{1,0:T(8,128)(2,1)}, bf16[64,256]{1,0:T(8,128)(2,1)S(1)}, u32[]{:S(2)}, u32[]{:S(2)}) collective-permute-start(bf16[64,256]{1,0:T(8,128)(2,1)} %get-tuple-element.58), channel_id=1, source_target_pairs={{0,12},{4,16},{8,20},{12,24},{16,28},{20,0},{24,4},{28,8},{1,13},{... | collective-permute-start | bytes 98312 | tf_op jit(solution)/shard_map/ppermute | solution.py:19
  36.9 0.5 collective-permute-start.10
  37.4 0.0 collective-permute-done.3.got_hbm
  37.4 0.9 %copy-done = bf16[1856,256]{1,0:T(8,128)(2,1)} copy-done((bf16[1856,256]{1,0:T(8,128)(2,1)}, bf16[1856,256]{1,0:T(8,128)(2,1)S(1)}, u32[]{:S(2)}) %copy-start) | copy-done | bytes 950296
  38.3 3.1 %chip_kv.1 = (f32[449,256]{1,0:T(8,128)}, bf16[464,256]{1,0:T(8,128)(2,1)}, bf16[464,256]{1,0:T(8,128)(2,1)}, bf16[464,256]{1,0:T(8,128)(2,1)}) custom-call(s32[1]{0:T(128)} %bitcast.1.chip_ref, bf16[1856,256]{1,0:T(8,128)(2,1)} %get-tuple-element.48.keep_hbm, bf16[1856,256]{1,0:T(8,128)(2,1)} %copy-done), custom_call_target="tpu_custom_call" | custom-call | tf_op jit(solution)/shard_map/chip_kv/pallas_call | solution.py:150
  41.4 0.0 copy-start.2
  41.4 0.0 collective-permute-done.7.refs_0_
  41.4 0.0 copy-start.3
  41.4 0.0 collective-permute-done.8.refs_1_
  41.4 0.0 copy-start.4
  41.4 0.0 collective-permute-done.9.refs_2_
  41.5 0.0 copy-start.5
  41.5 0.0 collective-permute-done.10.refs_3_
  41.5 0.6 copy-done.3
  42.0 0.0 copy-done.4
  42.0 0.0 copy-done.5
  42.1 0.6 copy-done.6
  42.7 4.7 %partial_proj.1 = (bf16[1856,256]{1,0:T(8,128)(2,1)}, bf16[1856,256]{1,0:T(8,128)(2,1)}) custom-call(s32[1]{0:T(128)} %bitcast.10.core_ref, bf16[256,3584]{1,0:T(8,128)(2,1)} %bitcast.17, bf16[64,256]{1,0:T(8,128)(2,1)} %copy-done.3, bf16[64,256]{1,0:T(8,128)(2,1)} %copy-done.4, bf16[64,256]{1,0:T(8,128)(2,1)} %copy-done.5, bf16[64,256]{1,0:T(8,128)(2,1)} %copy-done.6), custom_call_target="tpu_custom_call" | custom-call | tf_op jit(solution)/shard_map/partial_proj/pallas_call | solution.py:97
  47.4 0.1 collective-permute-start.11
  47.4 1.5 %collective-permute-start.4 = (bf16[464,256]{1,0:T(8,128)(2,1)}, bf16[464,256]{1,0:T(8,128)(2,1)S(1)}, u32[]{:S(2)}, u32[]{:S(2)}) collective-permute-start(bf16[464,256]{1,0:T(8,128)(2,1)} %get-tuple-element.52), channel_id=1, source_target_pairs={{0,8},{4,12},{8,16},{12,20},{16,24},{20,28},{24,0},{28,4},{1,9},{5... | collective-permute-start | bytes 712712 | tf_op jit(solution)/shard_map/ppermute | solution.py:19
  49.0 0.5 collective-permute-start.5
  49.5 2.4 %collective-permute-start.6 = (bf16[464,256]{1,0:T(8,128)(2,1)}, bf16[464,256]{1,0:T(8,128)(2,1)S(1)}, u32[]{:S(2)}, u32[]{:S(2)}) collective-permute-start(bf16[464,256]{1,0:T(8,128)(2,1)} %get-tuple-element.54), channel_id=1, source_target_pairs={{0,24},{4,28},{8,0},{12,4},{16,8},{20,12},{24,16},{28,20},{1,25},{... | collective-permute-start | bytes 712712 | tf_op jit(solution)/shard_map/ppermute | solution.py:19
  51.9 1.5 %maximum_bitcast_fusion = bf16[1,4,64,256]{3,2,1,0:T(8,128)(2,1)} fusion(bf16[1,64,256]{2,1,0:T(8,128)(2,1)} %bitcast.21, bf16[1,64,256]{2,1,0:T(8,128)(2,1)} %bitcast.20, bf16[1,64,256]{2,1,0:T(8,128)(2,1)} %bitcast.19, bf16[1,64,256]{2,1,0:T(8,128)(2,1)} %bitcast.18), kind=kLoop, calls=%fused_computation.2 | loop fusion | flops 196608 | bytes 262144 | tf_op jit(solution)/shard_map/broadcast_in_dim | solution.py:349
  53.4 3.9 %collective-permute-done.4 = bf16[464,256]{1,0:T(8,128)(2,1)S(1)} collective-permute-done((bf16[464,256]{1,0:T(8,128)(2,1)}, bf16[464,256]{1,0:T(8,128)(2,1)S(1)}, u32[]{:S(2)}, u32[]{:S(2)}) %collective-permute-start.4) | collective-permute-done | bytes 237600 | tf_op jit(solution)/shard_map/ppermute | solution.py:19
  57.3 4.5 %collective-permute-done.5 = bf16[464,256]{1,0:T(8,128)(2,1)S(1)} collective-permute-done((bf16[464,256]{1,0:T(8,128)(2,1)}, bf16[464,256]{1,0:T(8,128)(2,1)S(1)}, u32[]{:S(2)}, u32[]{:S(2)}) %collective-permute-start.5) | collective-permute-done | bytes 237600 | tf_op jit(solution)/shard_map/ppermute | solution.py:19
  61.8 0.1 collective-permute-done.6
  61.9 0.0 copy-done.2
  61.9 0.1 convert_add_fusion.1
  62.1 0.0 collective-permute-done.11.got_hbm
  62.1 0.0 copy-start.1
  62.1 0.9 %copy-done.1 = bf16[1856,256]{1,0:T(8,128)(2,1)} copy-done((bf16[1856,256]{1,0:T(8,128)(2,1)}, bf16[1856,256]{1,0:T(8,128)(2,1)S(1)}, u32[]{:S(2)}) %copy-start.1) | copy-done | bytes 950296
  63.0 3.1 %chip_proj.1 = (f32[449,256]{1,0:T(8,128)}, bf16[464,256]{1,0:T(8,128)(2,1)}, bf16[464,256]{1,0:T(8,128)(2,1)}, bf16[464,256]{1,0:T(8,128)(2,1)}) custom-call(s32[1]{0:T(128)} %bitcast.1.chip_ref, bf16[1856,256]{1,0:T(8,128)(2,1)} %get-tuple-element.60.keep_hbm, bf16[1856,256]{1,0:T(8,128)(2,1)} %copy-done.1), custom_call_target="tpu_custom_call" | custom-call | tf_op jit(solution)/shard_map/chip_proj/pallas_call | solution.py:150
  66.1 1.8 %collective-permute-start.12 = (bf16[464,256]{1,0:T(8,128)(2,1)}, bf16[464,256]{1,0:T(8,128)(2,1)S(1)}, u32[]{:S(2)}, u32[]{:S(2)}) collective-permute-start(bf16[464,256]{1,0:T(8,128)(2,1)} %get-tuple-element.63), channel_id=1, source_target_pairs={{0,8},{4,12},{8,16},{12,20},{16,24},{20,28},{24,0},{28,4},{1,9},{5... | collective-permute-start | bytes 712712 | tf_op jit(solution)/shard_map/ppermute | solution.py:19
  67.8 0.5 collective-permute-start.13
  68.3 1.4 %collective-permute-start.14 = (bf16[464,256]{1,0:T(8,128)(2,1)}, bf16[464,256]{1,0:T(8,128)(2,1)S(1)}, u32[]{:S(2)}, u32[]{:S(2)}) collective-permute-start(bf16[464,256]{1,0:T(8,128)(2,1)} %get-tuple-element.65), channel_id=1, source_target_pairs={{0,24},{4,28},{8,0},{12,4},{16,8},{20,12},{24,16},{28,20},{1,25},{... | collective-permute-start | bytes 712712 | tf_op jit(solution)/shard_map/ppermute | solution.py:19
  69.8 0.8 fusion
  70.6 5.3 %collective-permute-done.12 = bf16[464,256]{1,0:T(8,128)(2,1)S(1)} collective-permute-done((bf16[464,256]{1,0:T(8,128)(2,1)}, bf16[464,256]{1,0:T(8,128)(2,1)S(1)}, u32[]{:S(2)}, u32[]{:S(2)}) %collective-permute-start.12) | collective-permute-done | bytes 237600 | tf_op jit(solution)/shard_map/ppermute | solution.py:19
  75.9 4.0 %collective-permute-done.13 = bf16[464,256]{1,0:T(8,128)(2,1)S(1)} collective-permute-done((bf16[464,256]{1,0:T(8,128)(2,1)}, bf16[464,256]{1,0:T(8,128)(2,1)S(1)}, u32[]{:S(2)}, u32[]{:S(2)}) %collective-permute-start.13) | collective-permute-done | bytes 237600 | tf_op jit(solution)/shard_map/ppermute | solution.py:19
  79.9 0.0 collective-permute-done.14
  79.9 1.9 %convert_add_fusion = f32[449,256]{1,0:T(8,128)} fusion(f32[449,256]{1,0:T(8,128)} %get-tuple-element.62, bf16[464,256]{1,0:T(8,128)(2,1)S(1)} %collective-permute-done.14, bf16[464,256]{1,0:T(8,128)(2,1)S(1)} %collective-permute-done.13, bf16[464,256]{1,0:T(8,128)(2,1)S(1)} %collective-permute-done.12), kind=kLoop, calls=%fused_computation | loop fusion | flops 689664 | bytes 1609216 | tf_op jit(solution)/shard_map/add | solution.py:171
  (2 shorter events, 0.0 us)
Async XLA Ops:
  8.5 6.5 %copy-start.12 = (bf16[256,256]{1,0:T(8,128)(2,1)S(1)}, bf16[256,256]{1,0:T(8,128)(2,1)}, u32[]{:S(2)}) copy-start(bf16[256,256]{1,0:T(8,128)(2,1)} %get-tuple-element.40) | copy-start | bytes 393220
  8.5 9.2 %copy-start.11 = (bf16[256,256]{1,0:T(8,128)(2,1)S(1)}, bf16[256,256]{1,0:T(8,128)(2,1)}, u32[]{:S(2)}) copy-start(bf16[256,256]{1,0:T(8,128)(2,1)} %get-tuple-element.41) | copy-start | bytes 393220
  8.5 11.8 %copy-start.10 = (bf16[256,256]{1,0:T(8,128)(2,1)S(1)}, bf16[256,256]{1,0:T(8,128)(2,1)}, u32[]{:S(2)}) copy-start(bf16[256,256]{1,0:T(8,128)(2,1)} %get-tuple-element.42) | copy-start | bytes 393220
  14.5 22.9 %collective-permute-start.3 = (bf16[1856,256]{1,0:T(8,128)(2,1)}, bf16[1856,256]{1,0:T(8,128)(2,1)S(1)}, u32[]{:S(2)}, u32[]{:S(2)}) collective-permute-start(bf16[1856,256]{1,0:T(8,128)(2,1)} %get-tuple-element.49), channel_id=1, source_target_pairs={{0,4},{4,0},{8,12},{12,8},{16,20},{20,16},{24,28},{28,24},{1,5},{5... | collective-permute-start | bytes 2850824 | tf_op jit(solution)/shard_map/ppermute | solution.py:24
  15.1 9.1 %collective-permute-start = (bf16[256,256]{1,0:T(8,128)(2,1)S(1)}, bf16[256,256]{1,0:T(8,128)(2,1)S(1)}, u32[]{:S(2)}, u32[]{:S(2)}) collective-permute-start(bf16[256,256]{1,0:T(8,128)(2,1)S(1)} %copy-done.12), channel_id=1, source_target_pairs={{0,1},{1,2},{2,3},{3,0},{4,5},{5,6},{6,7},{7,4},{8,9},{9,10},{10,1... | collective-permute-start | bytes 393224 | tf_op jit(solution)/shard_map/ppermute | solution.py:19
  17.7 11.8 %collective-permute-start.1 = (bf16[256,256]{1,0:T(8,128)(2,1)S(1)}, bf16[256,256]{1,0:T(8,128)(2,1)S(1)}, u32[]{:S(2)}, u32[]{:S(2)}) collective-permute-start(bf16[256,256]{1,0:T(8,128)(2,1)S(1)} %copy-done.11), channel_id=1, source_target_pairs={{0,2},{1,3},{2,0},{3,1},{4,6},{5,7},{6,4},{7,5},{8,10},{9,11},{10,... | collective-permute-start | bytes 393224 | tf_op jit(solution)/shard_map/ppermute | solution.py:19
  20.3 9.2 %collective-permute-start.2 = (bf16[256,256]{1,0:T(8,128)(2,1)S(1)}, bf16[256,256]{1,0:T(8,128)(2,1)S(1)}, u32[]{:S(2)}, u32[]{:S(2)}) collective-permute-start(bf16[256,256]{1,0:T(8,128)(2,1)S(1)} %copy-done.10), channel_id=1, source_target_pairs={{0,3},{1,0},{2,1},{3,2},{4,7},{5,4},{6,5},{7,6},{8,11},{9,8},{10,9... | collective-permute-start | bytes 393224 | tf_op jit(solution)/shard_map/ppermute | solution.py:19
  24.2 5.3 %copy-start.7 = (bf16[256,256]{1,0:T(8,128)(2,1)}, bf16[256,256]{1,0:T(8,128)(2,1)S(1)}, u32[]{:S(2)}) copy-start(bf16[256,256]{1,0:T(8,128)(2,1)S(1)} %collective-permute-done.refs_0_) | copy-start | bytes 393220
  29.5 0.7 copy-start.8
  29.5 0.7 copy-start.9
  33.0 8.4 %collective-permute-start.7 = (bf16[64,256]{1,0:T(8,128)(2,1)}, bf16[64,256]{1,0:T(8,128)(2,1)S(1)}, u32[]{:S(2)}, u32[]{:S(2)}) collective-permute-start(bf16[64,256]{1,0:T(8,128)(2,1)} %get-tuple-element.56), channel_id=1, source_target_pairs={{0,4},{4,8},{8,12},{12,16},{16,20},{20,24},{24,28},{28,0},{1,5},{5... | collective-permute-start | bytes 98312 | tf_op jit(solution)/shard_map/ppermute | solution.py:19
  33.0 8.5 %collective-permute-start.8 = (bf16[64,256]{1,0:T(8,128)(2,1)}, bf16[64,256]{1,0:T(8,128)(2,1)S(1)}, u32[]{:S(2)}, u32[]{:S(2)}) collective-permute-start(bf16[64,256]{1,0:T(8,128)(2,1)} %get-tuple-element.57), channel_id=1, source_target_pairs={{0,8},{4,12},{8,16},{12,20},{16,24},{20,28},{24,0},{28,4},{1,9},{5... | collective-permute-start | bytes 98312 | tf_op jit(solution)/shard_map/ppermute | solution.py:19
  34.5 7.0 %collective-permute-start.9 = (bf16[64,256]{1,0:T(8,128)(2,1)}, bf16[64,256]{1,0:T(8,128)(2,1)S(1)}, u32[]{:S(2)}, u32[]{:S(2)}) collective-permute-start(bf16[64,256]{1,0:T(8,128)(2,1)} %get-tuple-element.58), channel_id=1, source_target_pairs={{0,12},{4,16},{8,20},{12,24},{16,28},{20,0},{24,4},{28,8},{1,13},{... | collective-permute-start | bytes 98312 | tf_op jit(solution)/shard_map/ppermute | solution.py:19
  36.9 4.6 %collective-permute-start.10 = (bf16[64,256]{1,0:T(8,128)(2,1)}, bf16[64,256]{1,0:T(8,128)(2,1)S(1)}, u32[]{:S(2)}, u32[]{:S(2)}) collective-permute-start(bf16[64,256]{1,0:T(8,128)(2,1)} %get-tuple-element.59), channel_id=1, source_target_pairs={{0,16},{4,20},{8,24},{12,28},{16,0},{20,4},{24,8},{28,12},{1,17},{... | collective-permute-start | bytes 98312 | tf_op jit(solution)/shard_map/ppermute | solution.py:19
  37.4 0.9 %copy-start = (bf16[1856,256]{1,0:T(8,128)(2,1)}, bf16[1856,256]{1,0:T(8,128)(2,1)S(1)}, u32[]{:S(2)}) copy-start(bf16[1856,256]{1,0:T(8,128)(2,1)S(1)} %collective-permute-done.3.got_hbm) | copy-start | bytes 2850820
  41.4 20.5 %copy-start.2 = (f32[449,256]{1,0:T(8,128)S(1)}, f32[449,256]{1,0:T(8,128)}, u32[]{:S(2)}) copy-start(f32[449,256]{1,0:T(8,128)} %get-tuple-element.51) | copy-start | bytes 1379332
  41.4 0.6 copy-start.3
  41.4 0.6 copy-start.4
  41.5 0.6 copy-start.5
  42.1 0.6 copy-start.6
  47.4 14.7 %collective-permute-start.11 = (bf16[1856,256]{1,0:T(8,128)(2,1)}, bf16[1856,256]{1,0:T(8,128)(2,1)S(1)}, u32[]{:S(2)}, u32[]{:S(2)}) collective-permute-start(bf16[1856,256]{1,0:T(8,128)(2,1)} %get-tuple-element.61), channel_id=1, source_target_pairs={{0,4},{4,0},{8,12},{12,8},{16,20},{20,16},{24,28},{28,24},{1,5},{5... | collective-permute-start | bytes 2850824 | tf_op jit(solution)/shard_map/ppermute | solution.py:24
  47.4 9.9 %collective-permute-start.4 = (bf16[464,256]{1,0:T(8,128)(2,1)}, bf16[464,256]{1,0:T(8,128)(2,1)S(1)}, u32[]{:S(2)}, u32[]{:S(2)}) collective-permute-start(bf16[464,256]{1,0:T(8,128)(2,1)} %get-tuple-element.52), channel_id=1, source_target_pairs={{0,8},{4,12},{8,16},{12,20},{16,24},{20,28},{24,0},{28,4},{1,9},{5... | collective-permute-start | bytes 712712 | tf_op jit(solution)/shard_map/ppermute | solution.py:19
  49.0 12.8 %collective-permute-start.5 = (bf16[464,256]{1,0:T(8,128)(2,1)}, bf16[464,256]{1,0:T(8,128)(2,1)S(1)}, u32[]{:S(2)}, u32[]{:S(2)}) collective-permute-start(bf16[464,256]{1,0:T(8,128)(2,1)} %get-tuple-element.53), channel_id=1, source_target_pairs={{0,16},{4,20},{8,24},{12,28},{16,0},{20,4},{24,8},{28,12},{1,17},{... | collective-permute-start | bytes 712712 | tf_op jit(solution)/shard_map/ppermute | solution.py:19
  49.5 12.4 %collective-permute-start.6 = (bf16[464,256]{1,0:T(8,128)(2,1)}, bf16[464,256]{1,0:T(8,128)(2,1)S(1)}, u32[]{:S(2)}, u32[]{:S(2)}) collective-permute-start(bf16[464,256]{1,0:T(8,128)(2,1)} %get-tuple-element.54), channel_id=1, source_target_pairs={{0,24},{4,28},{8,0},{12,4},{16,8},{20,12},{24,16},{28,20},{1,25},{... | collective-permute-start | bytes 712712 | tf_op jit(solution)/shard_map/ppermute | solution.py:19
  62.1 0.9 %copy-start.1 = (bf16[1856,256]{1,0:T(8,128)(2,1)}, bf16[1856,256]{1,0:T(8,128)(2,1)S(1)}, u32[]{:S(2)}) copy-start(bf16[1856,256]{1,0:T(8,128)(2,1)S(1)} %collective-permute-done.11.got_hbm) | copy-start | bytes 2850820
  66.1 9.8 %collective-permute-start.12 = (bf16[464,256]{1,0:T(8,128)(2,1)}, bf16[464,256]{1,0:T(8,128)(2,1)S(1)}, u32[]{:S(2)}, u32[]{:S(2)}) collective-permute-start(bf16[464,256]{1,0:T(8,128)(2,1)} %get-tuple-element.63), channel_id=1, source_target_pairs={{0,8},{4,12},{8,16},{12,20},{16,24},{20,28},{24,0},{28,4},{1,9},{5... | collective-permute-start | bytes 712712 | tf_op jit(solution)/shard_map/ppermute | solution.py:19
  67.8 12.0 %collective-permute-start.13 = (bf16[464,256]{1,0:T(8,128)(2,1)}, bf16[464,256]{1,0:T(8,128)(2,1)S(1)}, u32[]{:S(2)}, u32[]{:S(2)}) collective-permute-start(bf16[464,256]{1,0:T(8,128)(2,1)} %get-tuple-element.64), channel_id=1, source_target_pairs={{0,16},{4,20},{8,24},{12,28},{16,0},{20,4},{24,8},{28,12},{1,17},{... | collective-permute-start | bytes 712712 | tf_op jit(solution)/shard_map/ppermute | solution.py:19
  68.3 11.5 %collective-permute-start.14 = (bf16[464,256]{1,0:T(8,128)(2,1)}, bf16[464,256]{1,0:T(8,128)(2,1)S(1)}, u32[]{:S(2)}, u32[]{:S(2)}) collective-permute-start(bf16[464,256]{1,0:T(8,128)(2,1)} %get-tuple-element.65), channel_id=1, source_target_pairs={{0,24},{4,28},{8,0},{12,4},{16,8},{20,12},{24,16},{28,20},{1,25},{... | collective-permute-start | bytes 712712 | tf_op jit(solution)/shard_map/ppermute | solution.py:19

commit v3 on v2

--- a/solution.py
+++ b/solution.py
@@ -6,6 +6,7 @@
 from jax.experimental import pallas as pl
 from jax.experimental.pallas import tpu as pltpu
 from jax.sharding import PartitionSpec as P
+
 
 FEW = 8
 CHUNK = 512
@@ -145,7 +146,7 @@
         copy.wait()
 
 
-def chip_sums(keep, got, chips, rows, name):
+def chip_sums(keep, got, chips, rows):
     stride, cols = keep.shape[0] // chips, keep.shape[1]
     return pl.pallas_call(
         chip_sum_kernel,
@@ -160,7 +161,6 @@
             pltpu.SemaphoreType.DMA((chips, 2)),
             pltpu.SemaphoreType.DMA((max(chips - 1, 1),)),
         ],
-        name=name,
     )(scalar(lax.axis_index("dp") // 2), keep, got)
 
 
@@ -182,42 +182,58 @@
     return lax.psum_scatter(product, "dp", scatter_dimension=0, tiled=True)
 
 
-def encoder_kernel(me_ref, rows_ref, gain_ref, bias_ref, fc1_ref, b1_ref, fc2_ref, own_ref, *refs):
-    sends = refs[:-2]
-    normed, total = refs[-2:]
-    shards, _, cols = total.shape
-    step = pl.program_id(0)
-
-    @pl.when(step == 0)
-    def _():
-        values = rows_ref[...].astype(jnp.float32)
-        center = jnp.mean(values, axis=1, keepdims=True)
-        moved = values - center
-        spread_sq = jnp.mean(moved * moved, axis=1, keepdims=True)
-        normed[...] = (moved * lax.rsqrt(spread_sq + 1e-06) * gain_ref[...] + bias_ref[...]).astype(
+def encoder_kernel(
+    me_ref, rows_ref, gain_ref, bias_ref, b1_ref, fc1_hbm, fc2_hbm, own_hbm, *refs
+):
+    sends = refs[:-9]
+    fc1, fc2, normed, hidden, own, stage, in1_sem, in2_sem, out_sem = refs[-9:]
+    outs = (own_hbm,) + tuple(sends)
+    shards = len(outs)
+    cols = own.shape[1]
+    chunks, _, chunk = fc1.shape
+    order = list(range(1, shards)) + [0]
+    incoming1 = [
+        pltpu.make_async_copy(fc1_hbm.at[:, pl.ds(c * chunk, chunk)], fc1.at[c], in1_sem.at[c])
+        for c in range(chunks)
+    ]
+    incoming2 = []
+    for distance in order:
+        place = pl.multiple_of(lax.rem(me_ref[0] + distance, shards) * cols, 128)
+        incoming2.append(
+            pltpu.make_async_copy(
+                fc2_hbm.at[:, pl.ds(place, cols)], fc2.at[distance], in2_sem.at[distance]
+            )
+        )
+    for copy in incoming1 + incoming2:
+        copy.start()
+    values = rows_ref[...].astype(jnp.float32)
+    center = jnp.mean(values, axis=1, keepdims=True)
+    moved = values - center
+    spread_sq = jnp.mean(moved * moved, axis=1, keepdims=True)
+    normed[...] = (moved * lax.rsqrt(spread_sq + 1e-06) * gain_ref[...] + bias_ref[...]).astype(
+        jnp.bfloat16
+    )
+    for c in range(chunks):
+        incoming1[c].wait()
+        part = slice(c * chunk, (c + 1) * chunk)
+        before = jnp.dot(normed[...], fc1[c], preferred_element_type=jnp.float32) + b1_ref[:, part]
+        hidden[:, part] = (0.5 * before * (1.0 + lax.erf(before * 0.7071067811865476))).astype(
             jnp.bfloat16
         )
-
-    before = jnp.dot(normed[...], fc1_ref[...], preferred_element_type=jnp.float32) + b1_ref[...]
-    hidden = (0.5 * before * (1.0 + lax.erf(before * 0.7071067811865476))).astype(jnp.bfloat16)
-    for shard in range(shards):
-        piece = jnp.dot(
-            hidden, fc2_ref[:, shard * cols : (shard + 1) * cols], preferred_element_type=jnp.float32
-        )
-
-        @pl.when(step == 0)
-        def _(piece=piece, shard=shard):
-            total[shard] = piece
-
-        @pl.when(step > 0)
-        def _(piece=piece, shard=shard):
-            total[shard] += piece
-
-    @pl.when(step == pl.num_programs(0) - 1)
-    def _():
-        own_ref[...] = total[me_ref[0]]
-        for distance, send in enumerate(sends, 1):
-            send[...] = total[lax.rem(me_ref[0] + distance, shards)].astype(jnp.bfloat16)
+    leaving = []
+    for distance, copy in zip(order, incoming2):
+        copy.wait()
+        total = jnp.dot(hidden[...], fc2[distance], preferred_element_type=jnp.float32)
+        if distance == 0:
+            own[...] = total
+            source = own
+        else:
+            stage[distance] = total.astype(jnp.bfloat16)
+            source = stage.at[distance]
+        leaving.append(pltpu.make_async_copy(source, outs[distance], out_sem.at[distance]))
+        leaving[-1].start()
+    for copy in leaving:
+        copy.wait()
 
 
 def encoder_partials(rows, gain, bias, fc1, b1, fc2):
@@ -226,31 +242,25 @@
     units = fc1.shape[1]
     chunk = 256 if units % 256 == 0 else units
     cols = feats // shards
-    block = pl.BlockSpec((count, cols), lambda i, m: (0, 0))
-    line = pl.BlockSpec((1, feats), lambda i, m: (0, 0))
     return pl.pallas_call(
         encoder_kernel,
         out_shape=(jax.ShapeDtypeStruct((count, cols), jnp.float32),)
         + (jax.ShapeDtypeStruct((count, cols), jnp.bfloat16),) * (shards - 1),
-        grid_spec=pltpu.PrefetchScalarGridSpec(
-            num_scalar_prefetch=1,
-            grid=(units // chunk,),
-            in_specs=[
-                pl.BlockSpec((count, feats), lambda i, m: (0, 0)),
-                line,
-                line,
-                pl.BlockSpec((feats, chunk), lambda i, m: (0, i)),
-                pl.BlockSpec((1, chunk), lambda i, m: (0, i)),
-                pl.BlockSpec((chunk, feats), lambda i, m: (i, 0)),
-            ],
-            out_specs=(block,) * shards,
-            scratch_shapes=[
-                pltpu.VMEM((count, feats), jnp.bfloat16),
-                pltpu.VMEM((shards, count, cols), jnp.float32),
-            ],
-        ),
+        in_specs=[SMEM, VMEM, VMEM, VMEM, VMEM, ANY, ANY],
+        out_specs=(ANY,) * shards,
+        scratch_shapes=[
+            pltpu.VMEM((units // chunk, feats, chunk), jnp.bfloat16),
+            pltpu.VMEM((shards, units, cols), jnp.bfloat16),
+            pltpu.VMEM((count, feats), jnp.bfloat16),
+            pltpu.VMEM((count, units), jnp.bfloat16),
+            pltpu.VMEM((count, cols), jnp.float32),
+            pltpu.VMEM((shards, count, cols), jnp.bfloat16),
+            pltpu.SemaphoreType.DMA((units // chunk,)),
+            pltpu.SemaphoreType.DMA((shards,)),
+            pltpu.SemaphoreType.DMA((shards,)),
+        ],
         name="encoder",
-    )(scalar(lax.axis_index("mp")), rows, gain[None], bias[None], fc1, b1[None], fc2)
+    )(scalar(lax.axis_index("mp")), rows, gain[None], bias[None], b1[None], fc1, fc2)
 
 
 def pack_kernel(me_ref, counts_ref, offsets_ref, rows_ref, scale_ref, bias_ref, own_ref, *refs, spread):
@@ -299,7 +309,7 @@
     )(scalar(lax.axis_index("mp")), counts, offsets, rows, scale[None], bias[None], own, *parts)
 
 
-def per_device(
+def bucket(
     hidden_rows,
     key_grad,
     value_grad,
@@ -349,12 +359,12 @@
     handoff = jnp.stack(received, axis=0)[None]
     cotangent = visual_cotangent.reshape(spread * cap, width)
     if stepped:
-        kv_own, *kv_sends = chip_sums(kv_keep, kv_got, chips, rows, "chip_kv")
+        kv_own, *kv_sends = chip_sums(kv_keep, kv_got, chips, rows)
         cotangent, kv_own = lax.optimization_barrier((cotangent, kv_own))
         keep, send = partial_blocks(cotangent, received, ranks, rows, False)
         got = core_swap(send)
         kv_results = spread_sums(kv_own, kv_sends)
-        proj_own, *proj_sends = chip_sums(keep, got, chips, rows, "chip_proj")
+        proj_own, *proj_sends = chip_sums(keep, got, chips, rows)
         projector_grad = spread_sums(proj_own, proj_sends)
     else:
         kv_cotangent = jnp.concatenate([key_grad, value_grad], axis=1)
@@ -383,7 +393,7 @@
         P("dp", None),
     )
     return jax.shard_map(
-        per_device,
+        bucket,
         mesh=mesh,
         in_specs=placed,
         out_specs=(P("dp", "mp"), P("dp", "mp"), P("dp", "mp"), P("dp", None, None, "mp")),

time: 82.5 us -> 81 us (0.982)
  Pallas kernels: 27.4 us -> 25.8 us
    pallas_call x1, Pallas kernels: 7.89 us -> 6.31 us  [encoder_partials(): pl.pallas_call(encoder_kernel, out_shape=(jax.ShapeDtypeStruct((count, co...]
where the time goes in v3:
time: 81 us; the launch traced here: 80.2 us
  Pallas kernels  25.8 us (32%)
  waiting for transfers between devices  25.7 us (32%)
  starting transfers between devices  19.8 us (24%)
  local copies, waits for them, and re-layouts  4.58 us (6%)
  other arithmetic  3.52 us (4%)
  between operations  0.83 us (1%)
    ppermute x13, waiting for transfers between devices, shifted(): return lax.ppermute(x, axis, [(i, (i + by) % count) for i in range(count)])  25.7 us
    ppermute x13, starting transfers between devices, shifted(): return lax.ppermute(x, axis, [(i, (i + by) % count) for i in range(count)])  19.2 us
    pallas_call x2, Pallas kernels, partial_blocks(): pl.pallas_call(partial(partial_kernel, parts=len(rights), ranks=ranks, ro...  10.6 us
    pallas_call x1, Pallas kernels, encoder_partials(): pl.pallas_call(encoder_kernel, out_shape=(jax.ShapeDtypeStruct((count, co...  6.31 us
    pallas_call x2, Pallas kernels, chip_sums(): pl.pallas_call(chip_sum_kernel, in_specs=[SMEM, ANY, ANY], out_specs=(VME...  6.12 us
    unnamed x26, local copies, waits for them, and re-layouts  3.78 us
    pallas_call x1, Pallas kernels, packed_rows(): pl.pallas_call(partial(pack_kernel, spread=spread), out_shape=(jax.ShapeD...  2.75 us
    add x2, other arithmetic, spread_sums(): total + shifted(block, 'dp', 2 * distance)[:rows].astype(jnp.float32)  2.04 us
  transfers between devices with their start and end apart: 15, of which 7 were waited for; matrix products, arithmetic and copies ran while one was open for 3% of the time, Pallas kernels for 7%

profile of v3, /device:TPU:0, one launch (start us, length us, event | category | flops | bytes accessed | tf_op | source)
XLA Modules:
  0.0 80.2 jit_solution(15734982696715474887)
XLA Ops:
  0.6 6.3 %encoder.1 = (f32[256,256]{1,0:T(8,128)}, bf16[256,256]{1,0:T(8,128)(2,1)}, bf16[256,256]{1,0:T(8,128)(2,1)}, bf16[256,256]{1,0:T(8,128)(2,1)}) custom-call(s32[1]{0:T(128)} %bitcast.2.me_ref, bf16[256,1024]{1,0:T(8,128)(2,1)} %rows_ref.3, f32[1,1024]{1,0:T(1,128)} %bitcast.24, f32[1,1024]{1,0:T(1,128)} %bitcast.25, f32[1,1024]{1,0:T(1,128)} %bitcast.26, ...), custom_call_target="tpu_custom_call" | custom-call | tf_op jit(solution)/shard_map/encoder/pallas_call | solution.py:245
  7.0 0.0 copy-start.12
  7.0 0.0 copy-start.11
  7.0 0.0 copy-start.10
  7.0 5.9 %partial_kv.1 = (bf16[1856,256]{1,0:T(8,128)(2,1)}, bf16[1856,256]{1,0:T(8,128)(2,1)}) custom-call(s32[1]{0:T(128)} %bitcast.10.core_ref, bf16[512,3584]{1,0:T(8,128)(2,1)} %left_hbm, bf16[512,128]{1,0:T(8,128)(2,1)} %refs_0_.1, bf16[512,128]{1,0:T(8,128)(2,1)} %refs_1_.1), custom_call_target="tpu_custom_call" | custom-call | tf_op jit(solution)/shard_map/partial_kv/pallas_call | solution.py:98
  13.0 0.6 collective-permute-start.3
  13.5 0.0 copy-done.12
  13.5 2.6 %collective-permute-start = (bf16[256,256]{1,0:T(8,128)(2,1)S(1)}, bf16[256,256]{1,0:T(8,128)(2,1)S(1)}, u32[]{:S(2)}, u32[]{:S(2)}) collective-permute-start(bf16[256,256]{1,0:T(8,128)(2,1)S(1)} %copy-done.12), channel_id=1, source_target_pairs={{0,1},{1,2},{2,3},{3,0},{4,5},{5,6},{6,7},{7,4},{8,9},{9,10},{10,1... | collective-permute-start | bytes 393224 | tf_op jit(solution)/shard_map/ppermute | solution.py:20
  16.2 0.0 copy-done.11
  16.2 2.6 %collective-permute-start.1 = (bf16[256,256]{1,0:T(8,128)(2,1)S(1)}, bf16[256,256]{1,0:T(8,128)(2,1)S(1)}, u32[]{:S(2)}, u32[]{:S(2)}) collective-permute-start(bf16[256,256]{1,0:T(8,128)(2,1)S(1)} %copy-done.11), channel_id=1, source_target_pairs={{0,2},{1,3},{2,0},{3,1},{4,6},{5,7},{6,4},{7,5},{8,10},{9,11},{10,... | collective-permute-start | bytes 393224 | tf_op jit(solution)/shard_map/ppermute | solution.py:20
  18.7 0.0 copy-done.10
  18.7 1.3 %collective-permute-start.2 = (bf16[256,256]{1,0:T(8,128)(2,1)S(1)}, bf16[256,256]{1,0:T(8,128)(2,1)S(1)}, u32[]{:S(2)}, u32[]{:S(2)}) collective-permute-start(bf16[256,256]{1,0:T(8,128)(2,1)S(1)} %copy-done.10), channel_id=1, source_target_pairs={{0,3},{1,0},{2,1},{3,2},{4,7},{5,4},{6,5},{7,6},{8,11},{9,8},{10,9... | collective-permute-start | bytes 393224 | tf_op jit(solution)/shard_map/ppermute | solution.py:20
  20.1 2.5 %collective-permute-done.refs_0_ = bf16[256,256]{1,0:T(8,128)(2,1)S(1)} collective-permute-done((bf16[256,256]{1,0:T(8,128)(2,1)S(1)}, bf16[256,256]{1,0:T(8,128)(2,1)S(1)}, u32[]{:S(2)}, u32[]{:S(2)}) %collective-permute-start) | collective-permute-done | bytes 131104 | tf_op jit(solution)/shard_map/ppermute | solution.py:20
  22.6 0.0 copy-start.7
  22.6 5.3 %collective-permute-done.1.refs_1_ = bf16[256,256]{1,0:T(8,128)(2,1)S(1)} collective-permute-done((bf16[256,256]{1,0:T(8,128)(2,1)S(1)}, bf16[256,256]{1,0:T(8,128)(2,1)S(1)}, u32[]{:S(2)}, u32[]{:S(2)}) %collective-permute-start.1) | collective-permute-done | bytes 131104 | tf_op jit(solution)/shard_map/ppermute | solution.py:20
  28.0 0.0 copy-start.8
  28.0 0.0 collective-permute-done.2.refs_2_
  28.0 0.0 copy-start.9
  28.0 0.0 copy-done.7
  28.0 0.6 copy-done.8
  28.6 0.0 copy-done.9
  28.7 2.8 %pack.1 = (bf16[64,256]{1,0:T(8,128)(2,1)}, bf16[64,256]{1,0:T(8,128)(2,1)}, bf16[64,256]{1,0:T(8,128)(2,1)}, bf16[64,256]{1,0:T(8,128)(2,1)}) custom-call(s32[1]{0:T(128)} %bitcast.2.me_ref, s32[8]{0:T(128)} %bitcast.27, s32[8]{0:T(128)} %bitcast.28, bf16[256,1024]{1,0:T(8,128)(2,1)} %rows_ref.3, f32[1,1024]{1,0:T(1,128)} %bitcast.22, f32[1,1024]{1,0:T(1,128)} %bitcast.23, ...), custom_call_target="tpu_custom_call" | custom-call | tf_op jit(solution)/shard_map/pack/pallas_call | solution.py:298
  31.4 0.0 collective-permute-start.7
  31.4 1.5 %collective-permute-start.8 = (bf16[64,256]{1,0:T(8,128)(2,1)}, bf16[64,256]{1,0:T(8,128)(2,1)S(1)}, u32[]{:S(2)}, u32[]{:S(2)}) collective-permute-start(bf16[64,256]{1,0:T(8,128)(2,1)} %get-tuple-element.57), channel_id=1, source_target_pairs={{0,8},{4,12},{8,16},{12,20},{16,24},{20,28},{24,0},{28,4},{1,9},{5... | collective-permute-start | bytes 98312 | tf_op jit(solution)/shard_map/ppermute | solution.py:20
  32.9 2.4 %collective-permute-start.9 = (bf16[64,256]{1,0:T(8,128)(2,1)}, bf16[64,256]{1,0:T(8,128)(2,1)S(1)}, u32[]{:S(2)}, u32[]{:S(2)}) collective-permute-start(bf16[64,256]{1,0:T(8,128)(2,1)} %get-tuple-element.58), channel_id=1, source_target_pairs={{0,12},{4,16},{8,20},{12,24},{16,28},{20,0},{24,4},{28,8},{1,13},{... | collective-permute-start | bytes 98312 | tf_op jit(solution)/shard_map/ppermute | solution.py:20
  35.3 0.5 collective-permute-start.10
  35.8 0.0 collective-permute-done.3.got_hbm
  35.8 0.9 %copy-done = bf16[1856,256]{1,0:T(8,128)(2,1)} copy-done((bf16[1856,256]{1,0:T(8,128)(2,1)}, bf16[1856,256]{1,0:T(8,128)(2,1)S(1)}, u32[]{:S(2)}) %copy-start) | copy-done | bytes 950296
  36.8 3.1 %shard_map.165 = (f32[449,256]{1,0:T(8,128)}, bf16[464,256]{1,0:T(8,128)(2,1)}, bf16[464,256]{1,0:T(8,128)(2,1)}, bf16[464,256]{1,0:T(8,128)(2,1)}) custom-call(s32[1]{0:T(128)} %bitcast.1.chip_ref, bf16[1856,256]{1,0:T(8,128)(2,1)} %get-tuple-element.48.keep_hbm, bf16[1856,256]{1,0:T(8,128)(2,1)} %copy-done), custom_call_target="tpu_custom_call" | custom-call | tf_op jit(solution)/shard_map/pallas_call | solution.py:151
  39.9 0.0 copy-start.2
  39.9 0.0 collective-permute-done.7.refs_0_
  39.9 0.0 copy-start.3
  39.9 0.0 collective-permute-done.8.refs_1_
  39.9 0.0 copy-start.4
  39.9 0.0 collective-permute-done.9.refs_2_
  39.9 0.0 copy-start.5
  39.9 0.0 collective-permute-done.10.refs_3_
  39.9 0.6 copy-done.3
  40.5 0.0 copy-done.4
  40.5 0.0 copy-done.5
  40.5 0.6 copy-done.6
  41.1 4.7 %partial_proj.1 = (bf16[1856,256]{1,0:T(8,128)(2,1)}, bf16[1856,256]{1,0:T(8,128)(2,1)}) custom-call(s32[1]{0:T(128)} %bitcast.10.core_ref, bf16[256,3584]{1,0:T(8,128)(2,1)} %bitcast.17, bf16[64,256]{1,0:T(8,128)(2,1)} %copy-done.3, bf16[64,256]{1,0:T(8,128)(2,1)} %copy-done.4, bf16[64,256]{1,0:T(8,128)(2,1)} %copy-done.5, bf16[64,256]{1,0:T(8,128)(2,1)} %copy-done.6), custom_call_target="tpu_custom_call" | custom-call | tf_op jit(solution)/shard_map/partial_proj/pallas_call | solution.py:98
  45.8 0.1 collective-permute-start.11
  45.9 1.5 %collective-permute-start.4 = (bf16[464,256]{1,0:T(8,128)(2,1)}, bf16[464,256]{1,0:T(8,128)(2,1)S(1)}, u32[]{:S(2)}, u32[]{:S(2)}) collective-permute-start(bf16[464,256]{1,0:T(8,128)(2,1)} %get-tuple-element.52), channel_id=1, source_target_pairs={{0,8},{4,12},{8,16},{12,20},{16,24},{20,28},{24,0},{28,4},{1,9},{5... | collective-permute-start | bytes 712712 | tf_op jit(solution)/shard_map/ppermute | solution.py:20
  47.4 0.5 collective-permute-start.5
  47.9 2.4 %collective-permute-start.6 = (bf16[464,256]{1,0:T(8,128)(2,1)}, bf16[464,256]{1,0:T(8,128)(2,1)S(1)}, u32[]{:S(2)}, u32[]{:S(2)}) collective-permute-start(bf16[464,256]{1,0:T(8,128)(2,1)} %get-tuple-element.54), channel_id=1, source_target_pairs={{0,24},{4,28},{8,0},{12,4},{16,8},{20,12},{24,16},{28,20},{1,25},{... | collective-permute-start | bytes 712712 | tf_op jit(solution)/shard_map/ppermute | solution.py:20
  50.4 1.5 %maximum_bitcast_fusion = bf16[1,4,64,256]{3,2,1,0:T(8,128)(2,1)} fusion(bf16[1,64,256]{2,1,0:T(8,128)(2,1)} %bitcast.21, bf16[1,64,256]{2,1,0:T(8,128)(2,1)} %bitcast.20, bf16[1,64,256]{2,1,0:T(8,128)(2,1)} %bitcast.19, bf16[1,64,256]{2,1,0:T(8,128)(2,1)} %bitcast.18), kind=kLoop, calls=%fused_computation.2 | loop fusion | flops 196608 | bytes 262144 | tf_op jit(solution)/shard_map/broadcast_in_dim | solution.py:359
  51.9 3.9 %collective-permute-done.4 = bf16[464,256]{1,0:T(8,128)(2,1)S(1)} collective-permute-done((bf16[464,256]{1,0:T(8,128)(2,1)}, bf16[464,256]{1,0:T(8,128)(2,1)S(1)}, u32[]{:S(2)}, u32[]{:S(2)}) %collective-permute-start.4) | collective-permute-done | bytes 237600 | tf_op jit(solution)/shard_map/ppermute | solution.py:20
  55.8 4.5 %collective-permute-done.5 = bf16[464,256]{1,0:T(8,128)(2,1)S(1)} collective-permute-done((bf16[464,256]{1,0:T(8,128)(2,1)}, bf16[464,256]{1,0:T(8,128)(2,1)S(1)}, u32[]{:S(2)}, u32[]{:S(2)}) %collective-permute-start.5) | collective-permute-done | bytes 237600 | tf_op jit(solution)/shard_map/ppermute | solution.py:20
  60.3 0.1 collective-permute-done.6
  60.4 0.0 copy-done.2
  60.4 0.1 convert_add_fusion.1
  60.5 0.0 collective-permute-done.11.got_hbm
  60.5 0.0 copy-start.1
  60.5 0.9 %copy-done.1 = bf16[1856,256]{1,0:T(8,128)(2,1)} copy-done((bf16[1856,256]{1,0:T(8,128)(2,1)}, bf16[1856,256]{1,0:T(8,128)(2,1)S(1)}, u32[]{:S(2)}) %copy-start.1) | copy-done | bytes 950296
  61.5 3.1 %shard_map.166 = (f32[449,256]{1,0:T(8,128)}, bf16[464,256]{1,0:T(8,128)(2,1)}, bf16[464,256]{1,0:T(8,128)(2,1)}, bf16[464,256]{1,0:T(8,128)(2,1)}) custom-call(s32[1]{0:T(128)} %bitcast.1.chip_ref, bf16[1856,256]{1,0:T(8,128)(2,1)} %get-tuple-element.60.keep_hbm, bf16[1856,256]{1,0:T(8,128)(2,1)} %copy-done.1), custom_call_target="tpu_custom_call" | custom-call | tf_op jit(solution)/shard_map/pallas_call | solution.py:151
  64.5 1.8 %collective-permute-start.12 = (bf16[464,256]{1,0:T(8,128)(2,1)}, bf16[464,256]{1,0:T(8,128)(2,1)S(1)}, u32[]{:S(2)}, u32[]{:S(2)}) collective-permute-start(bf16[464,256]{1,0:T(8,128)(2,1)} %get-tuple-element.63), channel_id=1, source_target_pairs={{0,8},{4,12},{8,16},{12,20},{16,24},{20,28},{24,0},{28,4},{1,9},{5... | collective-permute-start | bytes 712712 | tf_op jit(solution)/shard_map/ppermute | solution.py:20
  66.3 0.5 collective-permute-start.13
  66.8 1.4 %collective-permute-start.14 = (bf16[464,256]{1,0:T(8,128)(2,1)}, bf16[464,256]{1,0:T(8,128)(2,1)S(1)}, u32[]{:S(2)}, u32[]{:S(2)}) collective-permute-start(bf16[464,256]{1,0:T(8,128)(2,1)} %get-tuple-element.65), channel_id=1, source_target_pairs={{0,24},{4,28},{8,0},{12,4},{16,8},{20,12},{24,16},{28,20},{1,25},{... | collective-permute-start | bytes 712712 | tf_op jit(solution)/shard_map/ppermute | solution.py:20
  68.2 0.8 fusion
  69.0 5.3 %collective-permute-done.12 = bf16[464,256]{1,0:T(8,128)(2,1)S(1)} collective-permute-done((bf16[464,256]{1,0:T(8,128)(2,1)}, bf16[464,256]{1,0:T(8,128)(2,1)S(1)}, u32[]{:S(2)}, u32[]{:S(2)}) %collective-permute-start.12) | collective-permute-done | bytes 237600 | tf_op jit(solution)/shard_map/ppermute | solution.py:20
  74.4 4.0 %collective-permute-done.13 = bf16[464,256]{1,0:T(8,128)(2,1)S(1)} collective-permute-done((bf16[464,256]{1,0:T(8,128)(2,1)}, bf16[464,256]{1,0:T(8,128)(2,1)S(1)}, u32[]{:S(2)}, u32[]{:S(2)}) %collective-permute-start.13) | collective-permute-done | bytes 237600 | tf_op jit(solution)/shard_map/ppermute | solution.py:20
  78.3 0.0 collective-permute-done.14
  78.3 1.9 %convert_add_fusion = f32[449,256]{1,0:T(8,128)} fusion(f32[449,256]{1,0:T(8,128)} %get-tuple-element.62, bf16[464,256]{1,0:T(8,128)(2,1)S(1)} %collective-permute-done.14, bf16[464,256]{1,0:T(8,128)(2,1)S(1)} %collective-permute-done.13, bf16[464,256]{1,0:T(8,128)(2,1)S(1)} %collective-permute-done.12), kind=kLoop, calls=%fused_computation | loop fusion | flops 689664 | bytes 1609216 | tf_op jit(solution)/shard_map/add | solution.py:171
  (2 shorter events, 0.0 us)
Async XLA Ops:
  7.0 6.6 %copy-start.12 = (bf16[256,256]{1,0:T(8,128)(2,1)S(1)}, bf16[256,256]{1,0:T(8,128)(2,1)}, u32[]{:S(2)}) copy-start(bf16[256,256]{1,0:T(8,128)(2,1)} %get-tuple-element.40) | copy-start | bytes 393220
  7.0 9.2 %copy-start.11 = (bf16[256,256]{1,0:T(8,128)(2,1)S(1)}, bf16[256,256]{1,0:T(8,128)(2,1)}, u32[]{:S(2)}) copy-start(bf16[256,256]{1,0:T(8,128)(2,1)} %get-tuple-element.41) | copy-start | bytes 393220
  7.0 11.8 %copy-start.10 = (bf16[256,256]{1,0:T(8,128)(2,1)S(1)}, bf16[256,256]{1,0:T(8,128)(2,1)}, u32[]{:S(2)}) copy-start(bf16[256,256]{1,0:T(8,128)(2,1)} %get-tuple-element.42) | copy-start | bytes 393220
  13.0 22.9 %collective-permute-start.3 = (bf16[1856,256]{1,0:T(8,128)(2,1)}, bf16[1856,256]{1,0:T(8,128)(2,1)S(1)}, u32[]{:S(2)}, u32[]{:S(2)}) collective-permute-start(bf16[1856,256]{1,0:T(8,128)(2,1)} %get-tuple-element.49), channel_id=1, source_target_pairs={{0,4},{4,0},{8,12},{12,8},{16,20},{20,16},{24,28},{28,24},{1,5},{5... | collective-permute-start | bytes 2850824 | tf_op jit(solution)/shard_map/ppermute | solution.py:25
  13.5 9.1 %collective-permute-start = (bf16[256,256]{1,0:T(8,128)(2,1)S(1)}, bf16[256,256]{1,0:T(8,128)(2,1)S(1)}, u32[]{:S(2)}, u32[]{:S(2)}) collective-permute-start(bf16[256,256]{1,0:T(8,128)(2,1)S(1)} %copy-done.12), channel_id=1, source_target_pairs={{0,1},{1,2},{2,3},{3,0},{4,5},{5,6},{6,7},{7,4},{8,9},{9,10},{10,1... | collective-permute-start | bytes 393224 | tf_op jit(solution)/shard_map/ppermute | solution.py:20
  16.2 11.8 %collective-permute-start.1 = (bf16[256,256]{1,0:T(8,128)(2,1)S(1)}, bf16[256,256]{1,0:T(8,128)(2,1)S(1)}, u32[]{:S(2)}, u32[]{:S(2)}) collective-permute-start(bf16[256,256]{1,0:T(8,128)(2,1)S(1)} %copy-done.11), channel_id=1, source_target_pairs={{0,2},{1,3},{2,0},{3,1},{4,6},{5,7},{6,4},{7,5},{8,10},{9,11},{10,... | collective-permute-start | bytes 393224 | tf_op jit(solution)/shard_map/ppermute | solution.py:20
  18.7 9.2 %collective-permute-start.2 = (bf16[256,256]{1,0:T(8,128)(2,1)S(1)}, bf16[256,256]{1,0:T(8,128)(2,1)S(1)}, u32[]{:S(2)}, u32[]{:S(2)}) collective-permute-start(bf16[256,256]{1,0:T(8,128)(2,1)S(1)} %copy-done.10), channel_id=1, source_target_pairs={{0,3},{1,0},{2,1},{3,2},{4,7},{5,4},{6,5},{7,6},{8,11},{9,8},{10,9... | collective-permute-start | bytes 393224 | tf_op jit(solution)/shard_map/ppermute | solution.py:20
  22.6 5.3 %copy-start.7 = (bf16[256,256]{1,0:T(8,128)(2,1)}, bf16[256,256]{1,0:T(8,128)(2,1)S(1)}, u32[]{:S(2)}) copy-start(bf16[256,256]{1,0:T(8,128)(2,1)S(1)} %collective-permute-done.refs_0_) | copy-start | bytes 393220
  28.0 0.7 copy-start.8
  28.0 0.7 copy-start.9
  31.4 8.5 %collective-permute-start.7 = (bf16[64,256]{1,0:T(8,128)(2,1)}, bf16[64,256]{1,0:T(8,128)(2,1)S(1)}, u32[]{:S(2)}, u32[]{:S(2)}) collective-permute-start(bf16[64,256]{1,0:T(8,128)(2,1)} %get-tuple-element.56), channel_id=1, source_target_pairs={{0,4},{4,8},{8,12},{12,16},{16,20},{20,24},{24,28},{28,0},{1,5},{5... | collective-permute-start | bytes 98312 | tf_op jit(solution)/shard_map/ppermute | solution.py:20
  31.4 8.5 %collective-permute-start.8 = (bf16[64,256]{1,0:T(8,128)(2,1)}, bf16[64,256]{1,0:T(8,128)(2,1)S(1)}, u32[]{:S(2)}, u32[]{:S(2)}) collective-permute-start(bf16[64,256]{1,0:T(8,128)(2,1)} %get-tuple-element.57), channel_id=1, source_target_pairs={{0,8},{4,12},{8,16},{12,20},{16,24},{20,28},{24,0},{28,4},{1,9},{5... | collective-permute-start | bytes 98312 | tf_op jit(solution)/shard_map/ppermute | solution.py:20
  32.9 7.0 %collective-permute-start.9 = (bf16[64,256]{1,0:T(8,128)(2,1)}, bf16[64,256]{1,0:T(8,128)(2,1)S(1)}, u32[]{:S(2)}, u32[]{:S(2)}) collective-permute-start(bf16[64,256]{1,0:T(8,128)(2,1)} %get-tuple-element.58), channel_id=1, source_target_pairs={{0,12},{4,16},{8,20},{12,24},{16,28},{20,0},{24,4},{28,8},{1,13},{... | collective-permute-start | bytes 98312 | tf_op jit(solution)/shard_map/ppermute | solution.py:20
  35.3 4.6 %collective-permute-start.10 = (bf16[64,256]{1,0:T(8,128)(2,1)}, bf16[64,256]{1,0:T(8,128)(2,1)S(1)}, u32[]{:S(2)}, u32[]{:S(2)}) collective-permute-start(bf16[64,256]{1,0:T(8,128)(2,1)} %get-tuple-element.59), channel_id=1, source_target_pairs={{0,16},{4,20},{8,24},{12,28},{16,0},{20,4},{24,8},{28,12},{1,17},{... | collective-permute-start | bytes 98312 | tf_op jit(solution)/shard_map/ppermute | solution.py:20
  35.8 0.9 %copy-start = (bf16[1856,256]{1,0:T(8,128)(2,1)}, bf16[1856,256]{1,0:T(8,128)(2,1)S(1)}, u32[]{:S(2)}) copy-start(bf16[1856,256]{1,0:T(8,128)(2,1)S(1)} %collective-permute-done.3.got_hbm) | copy-start | bytes 2850820
  39.9 20.5 %copy-start.2 = (f32[449,256]{1,0:T(8,128)S(1)}, f32[449,256]{1,0:T(8,128)}, u32[]{:S(2)}) copy-start(f32[449,256]{1,0:T(8,128)} %get-tuple-element.51) | copy-start | bytes 1379332
  39.9 0.6 copy-start.3
  39.9 0.6 copy-start.4
  39.9 0.6 copy-start.5
  40.5 0.6 copy-start.6
  45.8 14.7 %collective-permute-start.11 = (bf16[1856,256]{1,0:T(8,128)(2,1)}, bf16[1856,256]{1,0:T(8,128)(2,1)S(1)}, u32[]{:S(2)}, u32[]{:S(2)}) collective-permute-start(bf16[1856,256]{1,0:T(8,128)(2,1)} %get-tuple-element.61), channel_id=1, source_target_pairs={{0,4},{4,0},{8,12},{12,8},{16,20},{20,16},{24,28},{28,24},{1,5},{5... | collective-permute-start | bytes 2850824 | tf_op jit(solution)/shard_map/ppermute | solution.py:25
  45.9 9.9 %collective-permute-start.4 = (bf16[464,256]{1,0:T(8,128)(2,1)}, bf16[464,256]{1,0:T(8,128)(2,1)S(1)}, u32[]{:S(2)}, u32[]{:S(2)}) collective-permute-start(bf16[464,256]{1,0:T(8,128)(2,1)} %get-tuple-element.52), channel_id=1, source_target_pairs={{0,8},{4,12},{8,16},{12,20},{16,24},{20,28},{24,0},{28,4},{1,9},{5... | collective-permute-start | bytes 712712 | tf_op jit(solution)/shard_map/ppermute | solution.py:20
  47.4 12.8 %collective-permute-start.5 = (bf16[464,256]{1,0:T(8,128)(2,1)}, bf16[464,256]{1,0:T(8,128)(2,1)S(1)}, u32[]{:S(2)}, u32[]{:S(2)}) collective-permute-start(bf16[464,256]{1,0:T(8,128)(2,1)} %get-tuple-element.53), channel_id=1, source_target_pairs={{0,16},{4,20},{8,24},{12,28},{16,0},{20,4},{24,8},{28,12},{1,17},{... | collective-permute-start | bytes 712712 | tf_op jit(solution)/shard_map/ppermute | solution.py:20
  47.9 12.4 %collective-permute-start.6 = (bf16[464,256]{1,0:T(8,128)(2,1)}, bf16[464,256]{1,0:T(8,128)(2,1)S(1)}, u32[]{:S(2)}, u32[]{:S(2)}) collective-permute-start(bf16[464,256]{1,0:T(8,128)(2,1)} %get-tuple-element.54), channel_id=1, source_target_pairs={{0,24},{4,28},{8,0},{12,4},{16,8},{20,12},{24,16},{28,20},{1,25},{... | collective-permute-start | bytes 712712 | tf_op jit(solution)/shard_map/ppermute | solution.py:20
  60.5 0.9 %copy-start.1 = (bf16[1856,256]{1,0:T(8,128)(2,1)}, bf16[1856,256]{1,0:T(8,128)(2,1)S(1)}, u32[]{:S(2)}) copy-start(bf16[1856,256]{1,0:T(8,128)(2,1)S(1)} %collective-permute-done.11.got_hbm) | copy-start | bytes 2850820
  64.5 9.8 %collective-permute-start.12 = (bf16[464,256]{1,0:T(8,128)(2,1)}, bf16[464,256]{1,0:T(8,128)(2,1)S(1)}, u32[]{:S(2)}, u32[]{:S(2)}) collective-permute-start(bf16[464,256]{1,0:T(8,128)(2,1)} %get-tuple-element.63), channel_id=1, source_target_pairs={{0,8},{4,12},{8,16},{12,20},{16,24},{20,28},{24,0},{28,4},{1,9},{5... | collective-permute-start | bytes 712712 | tf_op jit(solution)/shard_map/ppermute | solution.py:20
  66.3 12.0 %collective-permute-start.13 = (bf16[464,256]{1,0:T(8,128)(2,1)}, bf16[464,256]{1,0:T(8,128)(2,1)S(1)}, u32[]{:S(2)}, u32[]{:S(2)}) collective-permute-start(bf16[464,256]{1,0:T(8,128)(2,1)} %get-tuple-element.64), channel_id=1, source_target_pairs={{0,16},{4,20},{8,24},{12,28},{16,0},{20,4},{24,8},{28,12},{1,17},{... | collective-permute-start | bytes 712712 | tf_op jit(solution)/shard_map/ppermute | solution.py:20
  66.8 11.5 %collective-permute-start.14 = (bf16[464,256]{1,0:T(8,128)(2,1)}, bf16[464,256]{1,0:T(8,128)(2,1)S(1)}, u32[]{:S(2)}, u32[]{:S(2)}) collective-permute-start(bf16[464,256]{1,0:T(8,128)(2,1)} %get-tuple-element.65), channel_id=1, source_target_pairs={{0,24},{4,28},{8,0},{12,4},{16,8},{20,12},{24,16},{28,20},{1,25},{... | collective-permute-start | bytes 712712 | tf_op jit(solution)/shard_map/ppermute | solution.py:20

commit v4 on v3

--- a/solution.py
+++ b/solution.py
@@ -333,15 +333,19 @@
     stepped = ranks <= FEW and ranks % 2 == 0
     chips = ranks // 2
 
+    first_rows = visual_rows
+    if stepped:
+        kv_keep, kv_send = partial_blocks(hidden_rows, (key_grad, value_grad), ranks, rows, True)
+        kv_got = core_swap(kv_send)
+        first_rows, kv_keep = lax.optimization_barrier((first_rows, kv_keep))
     own, *sends = encoder_partials(
-        visual_rows, norm_gain, norm_bias, fc1_weight, fc1_bias, fc2_weight
+        first_rows, norm_gain, norm_bias, fc1_weight, fc1_bias, fc2_weight
     )
     parts = [shifted(block, "mp", distance) for distance, block in enumerate(sends, 1)]
     if stepped:
-        left, own = lax.optimization_barrier((hidden_rows, own))
-        kv_keep, kv_send = partial_blocks(left, (key_grad, value_grad), ranks, rows, True)
-        kv_got = core_swap(kv_send)
         own, kv_keep = lax.optimization_barrier((own, kv_keep))
+        kv_own, *kv_sends = chip_sums(kv_keep, kv_got, chips, rows)
+        own, kv_own = lax.optimization_barrier((own, kv_own))
     packed = packed_rows(
         visual_rows,
         layer_scale,
@@ -353,14 +357,10 @@
         spread,
         cap,
     )
-    if stepped:
-        packed, kv_keep = lax.optimization_barrier((packed, kv_keep))
     received = [shifted(block, "dp", distance) for distance, block in enumerate(packed, 1)]
     handoff = jnp.stack(received, axis=0)[None]
     cotangent = visual_cotangent.reshape(spread * cap, width)
     if stepped:
-        kv_own, *kv_sends = chip_sums(kv_keep, kv_got, chips, rows)
-        cotangent, kv_own = lax.optimization_barrier((cotangent, kv_own))
         keep, send = partial_blocks(cotangent, received, ranks, rows, False)
         got = core_swap(send)
         kv_results = spread_sums(kv_own, kv_sends)

time: 81 us -> 79.2 us (0.978)
  transfers between devices with their start and end apart: 15 -> 15, of which waited for: 7 -> 9; matrix products, arithmetic and copies ran while one was open for 3% -> 3% of each run, Pallas kernels for 7% -> 12%
where the time goes in v4:
time: 79.2 us; the launch traced here: 78.3 us
  Pallas kernels  25.8 us (33%)
  waiting for transfers between devices  24.9 us (31%)
  starting transfers between devices  19.4 us (24%)
  local copies, waits for them, and re-layouts  3.99 us (5%)
  other arithmetic  3.52 us (4%)
  between operations  0.8 us (1%)
    ppermute x13, waiting for transfers between devices, shifted(): return lax.ppermute(x, axis, [(i, (i + by) % count) for i in range(count)])  24.9 us
    ppermute x13, starting transfers between devices, shifted(): return lax.ppermute(x, axis, [(i, (i + by) % count) for i in range(count)])  18.7 us
    pallas_call x2, Pallas kernels, partial_blocks(): pl.pallas_call(partial(partial_kernel, parts=len(rights), ranks=ranks, ro...  10.6 us
    pallas_call x1, Pallas kernels, encoder_partials(): pl.pallas_call(encoder_kernel, out_shape=(jax.ShapeDtypeStruct((count, co...  6.32 us
    pallas_call x2, Pallas kernels, chip_sums(): pl.pallas_call(chip_sum_kernel, in_specs=[SMEM, ANY, ANY], out_specs=(VME...  6.1 us
    unnamed x26, local copies, waits for them, and re-layouts  3.19 us
    pallas_call x1, Pallas kernels, packed_rows(): pl.pallas_call(partial(pack_kernel, spread=spread), out_shape=(jax.ShapeD...  2.77 us
    add x2, other arithmetic, spread_sums(): total + shifted(block, 'dp', 2 * distance)[:rows].astype(jnp.float32)  2.04 us
  transfers between devices with their start and end apart: 15, of which 9 were waited for; matrix products, arithmetic and copies ran while one was open for 3% of the time, Pallas kernels for 12%

profile of v4, /device:TPU:0, one launch (start us, length us, event | category | flops | bytes accessed | tf_op | source)
XLA Modules:
  0.0 78.3 jit_solution(6086144235773865365)
XLA Ops:
  0.6 5.9 %partial_kv.1 = (bf16[1856,256]{1,0:T(8,128)(2,1)}, bf16[1856,256]{1,0:T(8,128)(2,1)}) custom-call(s32[1]{0:T(128)} %bitcast.1.core_ref, bf16[512,3584]{1,0:T(8,128)(2,1)} %left_hbm.1, bf16[512,128]{1,0:T(8,128)(2,1)} %refs_0_.1, bf16[512,128]{1,0:T(8,128)(2,1)} %refs_1_.1), custom_call_target="tpu_custom_call" | custom-call | tf_op jit(solution)/shard_map/partial_kv/pallas_call | solution.py:98
  6.5 0.6 collective-permute-start
  7.1 6.3 %encoder.1 = (f32[256,256]{1,0:T(8,128)}, bf16[256,256]{1,0:T(8,128)(2,1)}, bf16[256,256]{1,0:T(8,128)(2,1)}, bf16[256,256]{1,0:T(8,128)(2,1)}) custom-call(s32[1]{0:T(128)} %bitcast.me_ref, bf16[256,1024]{1,0:T(8,128)(2,1)} %rows_ref.2, f32[1,1024]{1,0:T(1,128)} %bitcast.24, f32[1,1024]{1,0:T(1,128)} %bitcast.25, f32[1,1024]{1,0:T(1,128)} %bitcast.26, ...), custom_call_target="tpu_custom_call" | custom-call | tf_op jit(solution)/shard_map/encoder/pallas_call | solution.py:245
  13.4 2.6 %collective-permute-start.4 = (bf16[256,256]{1,0:T(8,128)(2,1)}, bf16[256,256]{1,0:T(8,128)(2,1)S(1)}, u32[]{:S(2)}, u32[]{:S(2)}) collective-permute-start(bf16[256,256]{1,0:T(8,128)(2,1)} %get-tuple-element.43), channel_id=1, source_target_pairs={{0,1},{1,2},{2,3},{3,0},{4,5},{5,6},{6,7},{7,4},{8,9},{9,10},{10,1... | collective-permute-start | bytes 393224 | tf_op jit(solution)/shard_map/ppermute | solution.py:20
  16.1 2.6 %collective-permute-start.5 = (bf16[256,256]{1,0:T(8,128)(2,1)}, bf16[256,256]{1,0:T(8,128)(2,1)S(1)}, u32[]{:S(2)}, u32[]{:S(2)}) collective-permute-start(bf16[256,256]{1,0:T(8,128)(2,1)} %get-tuple-element.44), channel_id=1, source_target_pairs={{0,2},{1,3},{2,0},{3,1},{4,6},{5,7},{6,4},{7,5},{8,10},{9,11},{10,... | collective-permute-start | bytes 393224 | tf_op jit(solution)/shard_map/ppermute | solution.py:20
  18.6 1.3 %collective-permute-start.6 = (bf16[256,256]{1,0:T(8,128)(2,1)}, bf16[256,256]{1,0:T(8,128)(2,1)S(1)}, u32[]{:S(2)}, u32[]{:S(2)}) collective-permute-start(bf16[256,256]{1,0:T(8,128)(2,1)} %get-tuple-element.45), channel_id=1, source_target_pairs={{0,3},{1,0},{2,1},{3,2},{4,7},{5,4},{6,5},{7,6},{8,11},{9,8},{10,9... | collective-permute-start | bytes 393224 | tf_op jit(solution)/shard_map/ppermute | solution.py:20
  20.0 0.0 collective-permute-done.got_hbm
  20.0 0.0 copy-start
  20.0 0.9 %copy-done = bf16[1856,256]{1,0:T(8,128)(2,1)} copy-done((bf16[1856,256]{1,0:T(8,128)(2,1)}, bf16[1856,256]{1,0:T(8,128)(2,1)S(1)}, u32[]{:S(2)}) %copy-start) | copy-done | bytes 950296
  20.9 3.0 %shard_map.165 = (f32[449,256]{1,0:T(8,128)}, bf16[464,256]{1,0:T(8,128)(2,1)}, bf16[464,256]{1,0:T(8,128)(2,1)}, bf16[464,256]{1,0:T(8,128)(2,1)}) custom-call(s32[1]{0:T(128)} %bitcast.5.chip_ref, bf16[1856,256]{1,0:T(8,128)(2,1)} %get-tuple-element.35.keep_hbm, bf16[1856,256]{1,0:T(8,128)(2,1)} %copy-done), custom_call_target="tpu_custom_call" | custom-call | tf_op jit(solution)/shard_map/pallas_call | solution.py:151
  24.0 0.0 copy-start.12
  24.0 0.0 copy-start.11
  24.0 0.0 copy-start.10
  24.0 0.0 copy-start.2
  24.0 0.0 collective-permute-done.4.refs_0_
  24.0 0.0 copy-start.7
  24.0 4.1 %collective-permute-done.5.refs_1_ = bf16[256,256]{1,0:T(8,128)(2,1)S(1)} collective-permute-done((bf16[256,256]{1,0:T(8,128)(2,1)}, bf16[256,256]{1,0:T(8,128)(2,1)S(1)}, u32[]{:S(2)}, u32[]{:S(2)}) %collective-permute-start.5) | collective-permute-done | bytes 131104 | tf_op jit(solution)/shard_map/ppermute | solution.py:20
  28.1 0.0 copy-start.8
  28.1 0.0 collective-permute-done.6.refs_2_
  28.1 0.0 copy-start.9
  28.1 0.0 copy-done.7
  28.1 0.6 copy-done.8
  28.8 0.0 copy-done.9
  28.8 2.8 %pack.1 = (bf16[64,256]{1,0:T(8,128)(2,1)}, bf16[64,256]{1,0:T(8,128)(2,1)}, bf16[64,256]{1,0:T(8,128)(2,1)}, bf16[64,256]{1,0:T(8,128)(2,1)}) custom-call(s32[1]{0:T(128)} %bitcast.me_ref, s32[8]{0:T(128)} %bitcast.27, s32[8]{0:T(128)} %bitcast.28, bf16[256,1024]{1,0:T(8,128)(2,1)} %rows_ref.2, f32[1,1024]{1,0:T(1,128)} %bitcast.22, f32[1,1024]{1,0:T(1,128)} %bitcast.23, ...), custom_call_target="tpu_custom_call" | custom-call | tf_op jit(solution)/shard_map/pack/pallas_call | solution.py:298
  31.6 0.0 collective-permute-start.7
  31.6 1.5 %collective-permute-start.8 = (bf16[64,256]{1,0:T(8,128)(2,1)}, bf16[64,256]{1,0:T(8,128)(2,1)S(1)}, u32[]{:S(2)}, u32[]{:S(2)}) collective-permute-start(bf16[64,256]{1,0:T(8,128)(2,1)} %get-tuple-element.47), channel_id=1, source_target_pairs={{0,8},{4,12},{8,16},{12,20},{16,24},{20,28},{24,0},{28,4},{1,9},{5... | collective-permute-start | bytes 98312 | tf_op jit(solution)/shard_map/ppermute | solution.py:20
  33.1 2.4 %collective-permute-start.9 = (bf16[64,256]{1,0:T(8,128)(2,1)}, bf16[64,256]{1,0:T(8,128)(2,1)S(1)}, u32[]{:S(2)}, u32[]{:S(2)}) collective-permute-start(bf16[64,256]{1,0:T(8,128)(2,1)} %get-tuple-element.48), channel_id=1, source_target_pairs={{0,12},{4,16},{8,20},{12,24},{16,28},{20,0},{24,4},{28,8},{1,13},{... | collective-permute-start | bytes 98312 | tf_op jit(solution)/shard_map/ppermute | solution.py:20
  35.5 0.5 collective-permute-start.10
  36.0 0.0 collective-permute-done.7.refs_0_
  36.0 0.0 copy-start.3
  36.0 0.6 collective-permute-done.8.refs_1_
  36.7 0.0 copy-start.4
  36.7 0.7 collective-permute-done.9.refs_2_
  37.4 2.2 %collective-permute-done.10.refs_3_ = bf16[64,256]{1,0:T(8,128)(2,1)S(1)} collective-permute-done((bf16[64,256]{1,0:T(8,128)(2,1)}, bf16[64,256]{1,0:T(8,128)(2,1)S(1)}, u32[]{:S(2)}, u32[]{:S(2)}) %collective-permute-start.10) | collective-permute-done | bytes 32800 | tf_op jit(solution)/shard_map/ppermute | solution.py:20
  39.6 0.0 copy-done.3
  39.6 0.0 copy-done.4
  39.6 0.0 copy-done.5
  39.6 0.6 copy-done.6
  40.2 4.7 %partial_proj.1 = (bf16[1856,256]{1,0:T(8,128)(2,1)}, bf16[1856,256]{1,0:T(8,128)(2,1)}) custom-call(s32[1]{0:T(128)} %bitcast.1.core_ref, bf16[256,3584]{1,0:T(8,128)(2,1)} %bitcast.17, bf16[64,256]{1,0:T(8,128)(2,1)} %copy-done.3, bf16[64,256]{1,0:T(8,128)(2,1)} %copy-done.4, bf16[64,256]{1,0:T(8,128)(2,1)} %copy-done.5, bf16[64,256]{1,0:T(8,128)(2,1)} %copy-done.6), custom_call_target="tpu_custom_call" | custom-call | tf_op jit(solution)/shard_map/partial_proj/pallas_call | solution.py:98
  44.9 0.1 collective-permute-start.11
  45.0 0.0 copy-done.12
  45.0 0.5 collective-permute-start.1
  45.5 0.0 copy-done.11
  45.5 1.5 %collective-permute-start.2 = (bf16[464,256]{1,0:T(8,128)(2,1)S(1)}, bf16[464,256]{1,0:T(8,128)(2,1)S(1)}, u32[]{:S(2)}, u32[]{:S(2)}) collective-permute-start(bf16[464,256]{1,0:T(8,128)(2,1)S(1)} %copy-done.11), channel_id=1, source_target_pairs={{0,16},{4,20},{8,24},{12,28},{16,0},{20,4},{24,8},{28,12},{1,17},{... | collective-permute-start | bytes 712712 | tf_op jit(solution)/shard_map/ppermute | solution.py:20
  47.1 0.0 copy-done.10
  47.1 1.4 %collective-permute-start.3 = (bf16[464,256]{1,0:T(8,128)(2,1)S(1)}, bf16[464,256]{1,0:T(8,128)(2,1)S(1)}, u32[]{:S(2)}, u32[]{:S(2)}) collective-permute-start(bf16[464,256]{1,0:T(8,128)(2,1)S(1)} %copy-done.10), channel_id=1, source_target_pairs={{0,24},{4,28},{8,0},{12,4},{16,8},{20,12},{24,16},{28,20},{1,25},{... | collective-permute-start | bytes 712712 | tf_op jit(solution)/shard_map/ppermute | solution.py:20
  48.5 1.5 %maximum_bitcast_fusion = bf16[1,4,64,256]{3,2,1,0:T(8,128)(2,1)} fusion(bf16[1,64,256]{2,1,0:T(8,128)(2,1)} %bitcast.21, bf16[1,64,256]{2,1,0:T(8,128)(2,1)} %bitcast.20, bf16[1,64,256]{2,1,0:T(8,128)(2,1)} %bitcast.19, bf16[1,64,256]{2,1,0:T(8,128)(2,1)} %bitcast.18), kind=kLoop, calls=%fused_computation.2 | loop fusion | flops 196608 | bytes 262144 | tf_op jit(solution)/shard_map/broadcast_in_dim | solution.py:361
  50.0 4.7 %collective-permute-done.1 = bf16[464,256]{1,0:T(8,128)(2,1)S(1)} collective-permute-done((bf16[464,256]{1,0:T(8,128)(2,1)S(1)}, bf16[464,256]{1,0:T(8,128)(2,1)S(1)}, u32[]{:S(2)}, u32[]{:S(2)}) %collective-permute-start.1) | collective-permute-done | bytes 237600 | tf_op jit(solution)/shard_map/ppermute | solution.py:20
  54.7 3.8 %collective-permute-done.2 = bf16[464,256]{1,0:T(8,128)(2,1)S(1)} collective-permute-done((bf16[464,256]{1,0:T(8,128)(2,1)S(1)}, bf16[464,256]{1,0:T(8,128)(2,1)S(1)}, u32[]{:S(2)}, u32[]{:S(2)}) %collective-permute-start.2) | collective-permute-done | bytes 237600 | tf_op jit(solution)/shard_map/ppermute | solution.py:20
  58.5 0.0 collective-permute-done.3
  58.5 0.0 copy-done.2
  58.5 0.1 convert_add_fusion.1
  58.6 0.0 collective-permute-done.11.got_hbm
  58.6 0.0 copy-start.1
  58.7 0.9 %copy-done.1 = bf16[1856,256]{1,0:T(8,128)(2,1)} copy-done((bf16[1856,256]{1,0:T(8,128)(2,1)}, bf16[1856,256]{1,0:T(8,128)(2,1)S(1)}, u32[]{:S(2)}) %copy-start.1) | copy-done | bytes 950296
  59.6 3.1 %shard_map.166 = (f32[449,256]{1,0:T(8,128)}, bf16[464,256]{1,0:T(8,128)(2,1)}, bf16[464,256]{1,0:T(8,128)(2,1)}, bf16[464,256]{1,0:T(8,128)(2,1)}) custom-call(s32[1]{0:T(128)} %bitcast.5.chip_ref, bf16[1856,256]{1,0:T(8,128)(2,1)} %get-tuple-element.50.keep_hbm, bf16[1856,256]{1,0:T(8,128)(2,1)} %copy-done.1), custom_call_target="tpu_custom_call" | custom-call | tf_op jit(solution)/shard_map/pallas_call | solution.py:151
  62.7 1.5 %collective-permute-start.12 = (bf16[464,256]{1,0:T(8,128)(2,1)}, bf16[464,256]{1,0:T(8,128)(2,1)S(1)}, u32[]{:S(2)}, u32[]{:S(2)}) collective-permute-start(bf16[464,256]{1,0:T(8,128)(2,1)} %get-tuple-element.53), channel_id=1, source_target_pairs={{0,8},{4,12},{8,16},{12,20},{16,24},{20,28},{24,0},{28,4},{1,9},{5... | collective-permute-start | bytes 712712 | tf_op jit(solution)/shard_map/ppermute | solution.py:20
  64.2 1.5 %collective-permute-start.13 = (bf16[464,256]{1,0:T(8,128)(2,1)}, bf16[464,256]{1,0:T(8,128)(2,1)S(1)}, u32[]{:S(2)}, u32[]{:S(2)}) collective-permute-start(bf16[464,256]{1,0:T(8,128)(2,1)} %get-tuple-element.54), channel_id=1, source_target_pairs={{0,16},{4,20},{8,24},{12,28},{16,0},{20,4},{24,8},{28,12},{1,17},{... | collective-permute-start | bytes 712712 | tf_op jit(solution)/shard_map/ppermute | solution.py:20
  65.7 1.2 %collective-permute-start.14 = (bf16[464,256]{1,0:T(8,128)(2,1)}, bf16[464,256]{1,0:T(8,128)(2,1)S(1)}, u32[]{:S(2)}, u32[]{:S(2)}) collective-permute-start(bf16[464,256]{1,0:T(8,128)(2,1)} %get-tuple-element.55), channel_id=1, source_target_pairs={{0,24},{4,28},{8,0},{12,4},{16,8},{20,12},{24,16},{28,20},{1,25},{... | collective-permute-start | bytes 712712 | tf_op jit(solution)/shard_map/ppermute | solution.py:20
  66.9 0.8 %fusion = (f32[449,128]{1,0:T(8,128)}, f32[449,128]{1,0:T(8,128)}) fusion(f32[449,256]{1,0:T(8,128)S(1)} %convert_add_fusion.1), kind=kLoop, calls=%fused_computation.3 | loop fusion | bytes 919552 | tf_op jit(solution)/shard_map/slice | solution.py:375
  67.7 4.8 %collective-permute-done.12 = bf16[464,256]{1,0:T(8,128)(2,1)S(1)} collective-permute-done((bf16[464,256]{1,0:T(8,128)(2,1)}, bf16[464,256]{1,0:T(8,128)(2,1)S(1)}, u32[]{:S(2)}, u32[]{:S(2)}) %collective-permute-start.12) | collective-permute-done | bytes 237600 | tf_op jit(solution)/shard_map/ppermute | solution.py:20
  72.5 3.4 %collective-permute-done.13 = bf16[464,256]{1,0:T(8,128)(2,1)S(1)} collective-permute-done((bf16[464,256]{1,0:T(8,128)(2,1)}, bf16[464,256]{1,0:T(8,128)(2,1)S(1)}, u32[]{:S(2)}, u32[]{:S(2)}) %collective-permute-start.13) | collective-permute-done | bytes 237600 | tf_op jit(solution)/shard_map/ppermute | solution.py:20
  76.0 0.5 collective-permute-done.14
  76.4 1.9 %convert_add_fusion = f32[449,256]{1,0:T(8,128)} fusion(f32[449,256]{1,0:T(8,128)} %get-tuple-element.52, bf16[464,256]{1,0:T(8,128)(2,1)S(1)} %collective-permute-done.14, bf16[464,256]{1,0:T(8,128)(2,1)S(1)} %collective-permute-done.13, bf16[464,256]{1,0:T(8,128)(2,1)S(1)} %collective-permute-done.12), kind=kLoop, calls=%fused_computation | loop fusion | flops 689664 | bytes 1609216 | tf_op jit(solution)/shard_map/add | solution.py:171
  (2 shorter events, 0.0 us)
Async XLA Ops:
  6.5 13.5 %collective-permute-start = (bf16[1856,256]{1,0:T(8,128)(2,1)}, bf16[1856,256]{1,0:T(8,128)(2,1)S(1)}, u32[]{:S(2)}, u32[]{:S(2)}) collective-permute-start(bf16[1856,256]{1,0:T(8,128)(2,1)} %get-tuple-element.36), channel_id=1, source_target_pairs={{0,4},{4,0},{8,12},{12,8},{16,20},{20,16},{24,28},{28,24},{1,5},{5... | collective-permute-start | bytes 2850824 | tf_op jit(solution)/shard_map/ppermute | solution.py:25
  13.4 10.6 %collective-permute-start.4 = (bf16[256,256]{1,0:T(8,128)(2,1)}, bf16[256,256]{1,0:T(8,128)(2,1)S(1)}, u32[]{:S(2)}, u32[]{:S(2)}) collective-permute-start(bf16[256,256]{1,0:T(8,128)(2,1)} %get-tuple-element.43), channel_id=1, source_target_pairs={{0,1},{1,2},{2,3},{3,0},{4,5},{5,6},{6,7},{7,4},{8,9},{9,10},{10,1... | collective-permute-start | bytes 393224 | tf_op jit(solution)/shard_map/ppermute | solution.py:20
  16.1 12.1 %collective-permute-start.5 = (bf16[256,256]{1,0:T(8,128)(2,1)}, bf16[256,256]{1,0:T(8,128)(2,1)S(1)}, u32[]{:S(2)}, u32[]{:S(2)}) collective-permute-start(bf16[256,256]{1,0:T(8,128)(2,1)} %get-tuple-element.44), channel_id=1, source_target_pairs={{0,2},{1,3},{2,0},{3,1},{4,6},{5,7},{6,4},{7,5},{8,10},{9,11},{10,... | collective-permute-start | bytes 393224 | tf_op jit(solution)/shard_map/ppermute | solution.py:20
  18.6 9.5 %collective-permute-start.6 = (bf16[256,256]{1,0:T(8,128)(2,1)}, bf16[256,256]{1,0:T(8,128)(2,1)S(1)}, u32[]{:S(2)}, u32[]{:S(2)}) collective-permute-start(bf16[256,256]{1,0:T(8,128)(2,1)} %get-tuple-element.45), channel_id=1, source_target_pairs={{0,3},{1,0},{2,1},{3,2},{4,7},{5,4},{6,5},{7,6},{8,11},{9,8},{10,9... | collective-permute-start | bytes 393224 | tf_op jit(solution)/shard_map/ppermute | solution.py:20
  20.0 0.9 %copy-start = (bf16[1856,256]{1,0:T(8,128)(2,1)}, bf16[1856,256]{1,0:T(8,128)(2,1)S(1)}, u32[]{:S(2)}) copy-start(bf16[1856,256]{1,0:T(8,128)(2,1)S(1)} %collective-permute-done.got_hbm) | copy-start | bytes 2850820
  24.0 21.0 %copy-start.12 = (bf16[464,256]{1,0:T(8,128)(2,1)S(1)}, bf16[464,256]{1,0:T(8,128)(2,1)}, u32[]{:S(2)}) copy-start(bf16[464,256]{1,0:T(8,128)(2,1)} %get-tuple-element.39) | copy-start | bytes 712708
  24.0 21.6 %copy-start.11 = (bf16[464,256]{1,0:T(8,128)(2,1)S(1)}, bf16[464,256]{1,0:T(8,128)(2,1)}, u32[]{:S(2)}) copy-start(bf16[464,256]{1,0:T(8,128)(2,1)} %get-tuple-element.40) | copy-start | bytes 712708
  24.0 23.1 %copy-start.10 = (bf16[464,256]{1,0:T(8,128)(2,1)S(1)}, bf16[464,256]{1,0:T(8,128)(2,1)}, u32[]{:S(2)}) copy-start(bf16[464,256]{1,0:T(8,128)(2,1)} %get-tuple-element.41) | copy-start | bytes 712708
  24.0 34.5 %copy-start.2 = (f32[449,256]{1,0:T(8,128)S(1)}, f32[449,256]{1,0:T(8,128)}, u32[]{:S(2)}) copy-start(f32[449,256]{1,0:T(8,128)} %get-tuple-element.38) | copy-start | bytes 1379332
  24.0 4.1 %copy-start.7 = (bf16[256,256]{1,0:T(8,128)(2,1)}, bf16[256,256]{1,0:T(8,128)(2,1)S(1)}, u32[]{:S(2)}) copy-start(bf16[256,256]{1,0:T(8,128)(2,1)S(1)} %collective-permute-done.4.refs_0_) | copy-start | bytes 393220
  28.1 0.7 copy-start.8
  28.1 0.7 copy-start.9
  31.6 4.4 %collective-permute-start.7 = (bf16[64,256]{1,0:T(8,128)(2,1)}, bf16[64,256]{1,0:T(8,128)(2,1)S(1)}, u32[]{:S(2)}, u32[]{:S(2)}) collective-permute-start(bf16[64,256]{1,0:T(8,128)(2,1)} %get-tuple-element.46), channel_id=1, source_target_pairs={{0,4},{4,8},{8,12},{12,16},{16,20},{20,24},{24,28},{28,0},{1,5},{5... | collective-permute-start | bytes 98312 | tf_op jit(solution)/shard_map/ppermute | solution.py:20
  31.6 5.1 %collective-permute-start.8 = (bf16[64,256]{1,0:T(8,128)(2,1)}, bf16[64,256]{1,0:T(8,128)(2,1)S(1)}, u32[]{:S(2)}, u32[]{:S(2)}) collective-permute-start(bf16[64,256]{1,0:T(8,128)(2,1)} %get-tuple-element.47), channel_id=1, source_target_pairs={{0,8},{4,12},{8,16},{12,20},{16,24},{20,28},{24,0},{28,4},{1,9},{5... | collective-permute-start | bytes 98312 | tf_op jit(solution)/shard_map/ppermute | solution.py:20
  33.1 4.3 %collective-permute-start.9 = (bf16[64,256]{1,0:T(8,128)(2,1)}, bf16[64,256]{1,0:T(8,128)(2,1)S(1)}, u32[]{:S(2)}, u32[]{:S(2)}) collective-permute-start(bf16[64,256]{1,0:T(8,128)(2,1)} %get-tuple-element.48), channel_id=1, source_target_pairs={{0,12},{4,16},{8,20},{12,24},{16,28},{20,0},{24,4},{28,8},{1,13},{... | collective-permute-start | bytes 98312 | tf_op jit(solution)/shard_map/ppermute | solution.py:20
  35.5 4.1 %collective-permute-start.10 = (bf16[64,256]{1,0:T(8,128)(2,1)}, bf16[64,256]{1,0:T(8,128)(2,1)S(1)}, u32[]{:S(2)}, u32[]{:S(2)}) collective-permute-start(bf16[64,256]{1,0:T(8,128)(2,1)} %get-tuple-element.49), channel_id=1, source_target_pairs={{0,16},{4,20},{8,24},{12,28},{16,0},{20,4},{24,8},{28,12},{1,17},{... | collective-permute-start | bytes 98312 | tf_op jit(solution)/shard_map/ppermute | solution.py:20
  36.0 3.6 %copy-start.3 = (bf16[64,256]{1,0:T(8,128)(2,1)}, bf16[64,256]{1,0:T(8,128)(2,1)S(1)}, u32[]{:S(2)}) copy-start(bf16[64,256]{1,0:T(8,128)(2,1)S(1)} %collective-permute-done.7.refs_0_) | copy-start | bytes 98308
  36.7 3.0 %copy-start.4 = (bf16[64,256]{1,0:T(8,128)(2,1)}, bf16[64,256]{1,0:T(8,128)(2,1)S(1)}, u32[]{:S(2)}) copy-start(bf16[64,256]{1,0:T(8,128)(2,1)S(1)} %collective-permute-done.8.refs_1_) | copy-start | bytes 98308
  37.4 2.2 %copy-start.5 = (bf16[64,256]{1,0:T(8,128)(2,1)}, bf16[64,256]{1,0:T(8,128)(2,1)S(1)}, u32[]{:S(2)}) copy-start(bf16[64,256]{1,0:T(8,128)(2,1)S(1)} %collective-permute-done.9.refs_2_) | copy-start | bytes 98308
  39.6 0.6 copy-start.6
  44.9 13.7 %collective-permute-start.11 = (bf16[1856,256]{1,0:T(8,128)(2,1)}, bf16[1856,256]{1,0:T(8,128)(2,1)S(1)}, u32[]{:S(2)}, u32[]{:S(2)}) collective-permute-start(bf16[1856,256]{1,0:T(8,128)(2,1)} %get-tuple-element.51), channel_id=1, source_target_pairs={{0,4},{4,0},{8,12},{12,8},{16,20},{20,16},{24,28},{28,24},{1,5},{5... | collective-permute-start | bytes 2850824 | tf_op jit(solution)/shard_map/ppermute | solution.py:25
  45.0 9.6 %collective-permute-start.1 = (bf16[464,256]{1,0:T(8,128)(2,1)S(1)}, bf16[464,256]{1,0:T(8,128)(2,1)S(1)}, u32[]{:S(2)}, u32[]{:S(2)}) collective-permute-start(bf16[464,256]{1,0:T(8,128)(2,1)S(1)} %copy-done.12), channel_id=1, source_target_pairs={{0,8},{4,12},{8,16},{12,20},{16,24},{20,28},{24,0},{28,4},{1,9},{5... | collective-permute-start | bytes 712712 | tf_op jit(solution)/shard_map/ppermute | solution.py:20
  45.5 12.9 %collective-permute-start.2 = (bf16[464,256]{1,0:T(8,128)(2,1)S(1)}, bf16[464,256]{1,0:T(8,128)(2,1)S(1)}, u32[]{:S(2)}, u32[]{:S(2)}) collective-permute-start(bf16[464,256]{1,0:T(8,128)(2,1)S(1)} %copy-done.11), channel_id=1, source_target_pairs={{0,16},{4,20},{8,24},{12,28},{16,0},{20,4},{24,8},{28,12},{1,17},{... | collective-permute-start | bytes 712712 | tf_op jit(solution)/shard_map/ppermute | solution.py:20
  47.1 11.4 %collective-permute-start.3 = (bf16[464,256]{1,0:T(8,128)(2,1)S(1)}, bf16[464,256]{1,0:T(8,128)(2,1)S(1)}, u32[]{:S(2)}, u32[]{:S(2)}) collective-permute-start(bf16[464,256]{1,0:T(8,128)(2,1)S(1)} %copy-done.10), channel_id=1, source_target_pairs={{0,24},{4,28},{8,0},{12,4},{16,8},{20,12},{24,16},{28,20},{1,25},{... | collective-permute-start | bytes 712712 | tf_op jit(solution)/shard_map/ppermute | solution.py:20
  58.6 0.9 %copy-start.1 = (bf16[1856,256]{1,0:T(8,128)(2,1)}, bf16[1856,256]{1,0:T(8,128)(2,1)S(1)}, u32[]{:S(2)}) copy-start(bf16[1856,256]{1,0:T(8,128)(2,1)S(1)} %collective-permute-done.11.got_hbm) | copy-start | bytes 2850820
  62.7 9.9 %collective-permute-start.12 = (bf16[464,256]{1,0:T(8,128)(2,1)}, bf16[464,256]{1,0:T(8,128)(2,1)S(1)}, u32[]{:S(2)}, u32[]{:S(2)}) collective-permute-start(bf16[464,256]{1,0:T(8,128)(2,1)} %get-tuple-element.53), channel_id=1, source_target_pairs={{0,8},{4,12},{8,16},{12,20},{16,24},{20,28},{24,0},{28,4},{1,9},{5... | collective-permute-start | bytes 712712 | tf_op jit(solution)/shard_map/ppermute | solution.py:20
  64.2 11.8 %collective-permute-start.13 = (bf16[464,256]{1,0:T(8,128)(2,1)}, bf16[464,256]{1,0:T(8,128)(2,1)S(1)}, u32[]{:S(2)}, u32[]{:S(2)}) collective-permute-start(bf16[464,256]{1,0:T(8,128)(2,1)} %get-tuple-element.54), channel_id=1, source_target_pairs={{0,16},{4,20},{8,24},{12,28},{16,0},{20,4},{24,8},{28,12},{1,17},{... | collective-permute-start | bytes 712712 | tf_op jit(solution)/shard_map/ppermute | solution.py:20
  65.7 10.7 %collective-permute-start.14 = (bf16[464,256]{1,0:T(8,128)(2,1)}, bf16[464,256]{1,0:T(8,128)(2,1)S(1)}, u32[]{:S(2)}, u32[]{:S(2)}) collective-permute-start(bf16[464,256]{1,0:T(8,128)(2,1)} %get-tuple-element.55), channel_id=1, source_target_pairs={{0,24},{4,28},{8,0},{12,4},{16,8},{20,12},{24,16},{28,20},{1,25},{... | collective-permute-start | bytes 712712 | tf_op jit(solution)/shard_map/ppermute | solution.py:20
